TPU v7x, 512 devices: a whole 4x8x8 slice. The times are simulated.
512 devices in a mesh: dp: 4 (over z_hi), pipe: 4 (over z_lo, core), sg: 32 (over y, x).
Axes of the slice: x: 4, y: 8, z: 8 (z_hi: 4, z_lo: 2; z = z_hi * 2 + z_lo), core: 2. Of those that a mesh axis runs over, the one named last changes fastest.
Arguments:
- inputs: bfloat16 [4, 4, 32, 16, 16, 256], P('pipe', 'dp', 'sg'), may hold values from -6 to 6
- cotangent: bfloat16 [4, 4, 32, 16, 16, 256], P('pipe', 'dp', 'sg'), may hold values from -6 to 6
- w_in: bfloat16 [4, 256, 256], P('pipe'), may hold values from -0.375 to 0.375
- w_out: bfloat16 [4, 256, 256], P('pipe'), may hold values from -0.375 to 0.375
- w_group: bfloat16 [4, 3, 3, 3, 8, 256], P('pipe'), may hold values from -0.4375 to 0.4375
Outputs:
- section_grad: bfloat16 [4, 4, 32, 16, 16, 256], P('pipe', 'dp', 'sg')
- grad_in: float32 [4, 256, 256], P('pipe', ('dp', 'sg'))
- grad_out: float32 [4, 256, 256], P('pipe', ('dp', 'sg'))
- grad_group: float32 [4, 3, 3, 3, 8, 256], P('pipe', None, None, None, None, 'sg')
All inputs are finite; a program needn't handle non-finite values.
Results may differ from a plain program's by a relative error of at most 0.0065.
Values may be sent and summed in bfloat16 or wider, within the bound.
No kernel may reach another device: no remote copies, remote signals or barrier semaphores. Data moves between devices by JAX's collectives and lax.ppermute only.
A program may use at most 64 MiB of HBM per device.

v0:
```python
import jax
import jax.numpy as jnp
from jax import lax
from jax.sharding import PartitionSpec as P


def shifted_2(value, axis, steps):
    count = lax.axis_size(axis)
    initial, last = (max(0, -steps), min(count, count - steps))
    return lax.ppermute(value, axis, [(source, source + steps) for source in range(initial, last)])


def silu_slope(value):
    sigmoid_value = jax.nn.sigmoid(value)
    return sigmoid_value * (1.0 + value * (1.0 - sigmoid_value))


def shifted(padded, first, second, third, side):
    depth = padded.shape[3] - 2
    planes = padded[:, :, :, first : first + depth, :]
    wide = jnp.pad(planes, ((0, 0), (0, 0), (0, 0), (0, 0), (side + 1, side + 1)))
    start = side + 1 + (second - 1) * side + (third - 1)
    piece = wide[:, :, :, :, start : start + side * side]
    column = lax.iota(jnp.int32, side * side) % side + (third - 1)
    valid = (column >= 0) & (column < side)
    return jnp.where(valid, piece, jnp.zeros_like(piece))


def conv_forward(padded, kernel, side):
    group_width = kernel.shape[3]
    local_groups = kernel.shape[4] // group_width
    split_kernel = kernel.reshape(3, 3, 3, group_width, local_groups, group_width)
    total = None
    for first in range(3):
        for second in range(3):
            for third in range(3):
                piece = shifted(padded, first, second, third, side)
                term = jnp.einsum(
                    "gibdn,igo->gobdn",
                    piece,
                    split_kernel[first, second, third],
                    preferred_element_type=jnp.float32,
                )
                total = term if total is None else total + term
    return total


def conv_backward(padded, kernel, side):
    group_width = kernel.shape[3]
    local_groups = kernel.shape[4] // group_width
    split_kernel = kernel.reshape(3, 3, 3, group_width, local_groups, group_width)
    total = None
    for first in range(3):
        for second in range(3):
            for third in range(3):
                piece = shifted(padded, 2 - first, 2 - second, 2 - third, side)
                term = jnp.einsum(
                    "gobdn,igo->gibdn",
                    piece,
                    split_kernel[first, second, third],
                    preferred_element_type=jnp.float32,
                )
                total = term if total is None else total + term
    return total


def kernel_grad(padded, slopes, side):
    local_groups, group_width = (slopes.shape[0], slopes.shape[1])
    terms = []
    for first in range(3):
        for second in range(3):
            for third in range(3):
                piece = shifted(padded, first, second, third, side)
                block = jnp.einsum(
                    "gibdn,gobdn->igo", piece, slopes, preferred_element_type=jnp.float32
                )
                terms.append(block.reshape(group_width, local_groups * group_width))
    return jnp.stack(terms).reshape(3, 3, 3, group_width, local_groups * group_width)


def pad_depth(volume):
    return jnp.pad(volume, ((0, 0), (0, 0), (0, 0), (1, 1), (0, 0)))


def per_device(inputs, cotangent, w_in, w_out, w_group):
    channels = inputs.shape[-1]
    samples, planes, side = (inputs.shape[1], inputs.shape[2], inputs.shape[3])
    group_width = w_group.shape[4]
    cells = side * side
    shape = inputs.shape
    rows_in = inputs.reshape(-1, channels)
    rows_grad = cotangent.reshape(-1, channels)
    pre_first = jnp.einsum("nc,ce->en", rows_in, w_in[0], preferred_element_type=jnp.float32)
    first_act = (
        jax.nn.silu(pre_first).astype(jnp.bfloat16).reshape(channels, samples, planes, cells)
    )
    back_second = (
        jnp.einsum("nd,cd->cn", rows_grad, w_out[0], preferred_element_type=jnp.float32)
        .astype(jnp.bfloat16)
        .reshape(channels, samples, planes, cells)
    )
    first_grp, back_grp = (
        lax.all_to_all(first_act, "sg", split_axis=0, concat_axis=2, tiled=True),
        lax.all_to_all(back_second, "sg", split_axis=0, concat_axis=2, tiled=True),
    )
    local_width = channels // lax.axis_size("sg")
    local_groups = local_width // group_width
    depth = first_grp.shape[2]
    kernel = lax.dynamic_slice_in_dim(
        w_group[0], lax.axis_index("sg") * local_width, local_width, 4
    )
    padded = pad_depth(first_grp.reshape(local_groups, group_width, samples, depth, cells))
    pre_second = conv_forward(padded, kernel, side)
    second_act = jax.nn.silu(pre_second).astype(jnp.bfloat16)
    slopes = (
        back_grp.reshape(pre_second.shape).astype(jnp.float32) * silu_slope(pre_second)
    ).astype(jnp.bfloat16)
    second_slab = lax.all_to_all(
        second_act.reshape(local_width, samples, depth, cells),
        "sg",
        split_axis=2,
        concat_axis=0,
        tiled=True,
    )
    kernel_part = kernel_grad(padded, slopes, side)
    back_first = conv_backward(pad_depth(slopes), kernel, side).astype(jnp.bfloat16)
    back_slab = lax.all_to_all(
        back_first.reshape(local_width, samples, depth, cells),
        "sg",
        split_axis=2,
        concat_axis=0,
        tiled=True,
    )
    kernel_total = lax.psum(kernel_part, "dp")[None]
    second_rows = second_slab.reshape(channels, -1)
    grad_out_part = jnp.einsum(
        "cn,nd->cd", second_rows, rows_grad, preferred_element_type=jnp.float32
    )
    slope_first = (
        back_slab.reshape(channels, -1).astype(jnp.float32) * silu_slope(pre_first)
    ).astype(jnp.bfloat16)
    grad_in_part = jnp.einsum("nc,dn->cd", rows_in, slope_first, preferred_element_type=jnp.float32)
    back_input = rows_grad.astype(jnp.float32) + jnp.einsum(
        "dn,cd->nc", slope_first, w_in[0], preferred_element_type=jnp.float32
    )
    back_input = back_input.astype(jnp.bfloat16).reshape(shape)
    section_grad = shifted_2(back_input, "pipe", -1)
    grad_in, grad_out = (
        lax.psum_scatter(grad_in_part[None], ("dp", "sg"), scatter_dimension=1, tiled=True),
        lax.psum_scatter(grad_out_part[None], ("dp", "sg"), scatter_dimension=1, tiled=True),
    )
    return (section_grad, grad_in, grad_out, kernel_total)


def solution(mesh):
    placed = (
        P("pipe", "dp", "sg", None, None, None),
        P("pipe", "dp", "sg", None, None, None),
        P("pipe", None, None),
        P("pipe", None, None),
        P("pipe", None, None, None, None, None),
    )
    return jax.shard_map(
        per_device,
        mesh=mesh,
        in_specs=placed,
        out_specs=(
            P("pipe", "dp", "sg", None, None, None),
            P("pipe", ("dp", "sg"), None),
            P("pipe", ("dp", "sg"), None),
            P("pipe", None, None, None, None, "sg"),
        ),
        check_vma=False,
    )
```

profile of v0, /device:TPU:2, one launch (start us, length us, event | category | flops | bytes accessed | tf_op | source)
XLA Modules:
  0.0 1444.4 jit_solution(7984702821594910338)
XLA Ops:
  7.2 0.9 copy-done
  8.1 1.1 fusion.136
  9.3 0.5 broadcast.480
  9.8 0.7 reduce.1
  10.5 0.7 reshape.800
  11.2 10.4 all-to-all-start.1
  21.9 0.7 reduce
  22.5 0.7 reshape.798
  23.3 1.3 dynamic-slice.1
  25.3 5.1 all-to-all-done.1
  30.4 5.3 all-to-all-start
  36.2 0.2 convolution_add_fusion.52
  36.7 0.2 convolution_add_fusion.50
  37.2 0.2 convolution_add_fusion.48
  37.7 0.2 convolution_add_fusion.46
  37.9 0.2 convolution_add_fusion.45
  38.4 0.2 convolution_add_fusion.43
  38.6 0.2 convolution_add_fusion.42
  39.6 0.2 convolution_add_fusion.38
  39.9 0.2 convolution_add_fusion.37
  40.4 0.2 convolution_add_fusion.35
  40.6 0.2 convolution_add_fusion.34
  42.3 2.4 all-to-all-done
  44.8 0.3 convert_element_type.160
  45.1 1.0 fusion.143
  46.1 0.3 convolution_bitcast_fusion.28
  46.3 0.3 convolution_bitcast_fusion.27
  46.6 0.3 convolution_bitcast_fusion.26
  46.9 0.3 convolution_bitcast_fusion.25
  47.4 0.3 convolution_bitcast_fusion.23
  47.7 0.3 convolution_bitcast_fusion.22
  48.0 0.3 convolution_bitcast_fusion.21
  48.2 0.3 convolution_bitcast_fusion.20
  48.5 0.3 convolution_bitcast_fusion.19
  48.8 0.3 convolution_bitcast_fusion.18
  49.1 0.3 convolution_bitcast_fusion.17
  49.4 0.3 convolution_bitcast_fusion.16
  49.9 0.3 convolution_bitcast_fusion.14
  50.1 0.3 convolution_bitcast_fusion.13
  50.4 0.3 convolution_bitcast_fusion.12
  50.7 0.3 convolution_bitcast_fusion.11
  51.0 0.3 convolution_bitcast_fusion.10
  51.3 0.3 convolution_bitcast_fusion.9
  51.6 0.3 convolution_bitcast_fusion.8
  51.9 0.3 convolution_bitcast_fusion.7
  52.3 0.3 convolution_bitcast_fusion.5
  52.6 0.3 convolution_bitcast_fusion.4
  52.9 0.3 convolution_bitcast_fusion.3
  61.0 0.9 fusion.3
  61.8 7.5 all-to-all-start.2
  69.7 0.3 convolution_bitcast_fusion.2
  69.9 8.2 all-to-all-done.2
  78.2 5.6 all-to-all-start.3
  84.1 0.8 copy.270
  84.9 7.8 all-to-all-done.3
  92.7 0.9 convolution_bitcast_fusion
  93.7 0.8 copy-done.2
  94.7 1.3 collective-permute-start
  96.0 27.1 %psum.7 = f32[1,3,3,3,8,8]{5,4,3,2,1,0:T(8,128)} all-reduce(f32[1,3,3,3,8,8]{5,4,3,2,1,0:T(8,128)S(1)} %bitcast.714), channel_id=1, replica_groups=mesh['dp'=4,'pipe'=4,'sg'=32] {'dp'}, use_global_device_ids=true, to_apply=%region_2.3 | all-reduce | flops 1728 | bytes 13824 | tf_op jit(solution)/shard_map/psum | solution.py:134
  123.1 1311.2 %all-reduce.13.cloned.1.call-done = (f32[1,256,256]{2,0,1:T(1,128)}, f32[1,256,256]{2,1,0:T(8,128)}) async-done(((f32[1,256,256]{2,0,1:T(1,128)}, f32[1,256,256]{2,1,0:T(8,128)}), (f32[1,256,256]{2,0,1:T(1,128)}, f32[1,256,256]{2,1,0:T(8,128)})) %all-reduce.13.cloned.1.call-update) | async-done | bytes 524304
  1434.3 0.7 constant_dynamic-slice_fusion.1
  1435.0 0.6 copy.299
  1435.6 1.3 constant_dynamic-slice_fusion
  1436.9 0.7 copy.400
  (123 shorter events, 13.2 us)
Async XLA Ops:
  7.2 0.9 copy-start
  11.2 10.4 copy-start.1
  11.2 10.4 copy-start.3
  11.2 19.2 %all-to-all-start.1 = ((bf16[32,2,1024]{2,1,0:T(2,128)(2,1)}), bf16[32,2,1024]{2,1,0:T(2,128)(2,1)S(1)}, u32[]{:S(2)}, u32[]{:S(2)}) async-start(bf16[32,2,1024]{2,1,0:T(2,128)(2,1)} %reshape.800), calls=%async_computation.1 | async-start | bytes 262144 | tf_op jit(solution)/shard_map/all_to_all | solution.py:103
  22.5 2.7 copy-start.4
  30.4 14.3 all-to-all-start
  61.8 16.3 %all-to-all-start.2 = ((bf16[8,1,32,256]{3,0,1,2:T(8,128)(2,1)}), bf16[8,1,32,256]{3,0,1,2:T(8,128)(2,1)S(1)}, u32[]{:S(2)}, u32[]{:S(2)}) async-start(bf16[8,1,32,256]{3,0,1,2:T(8,128)(2,1)} %fusion.3), calls=%async_computation.2 | async-start | bytes 262144 | tf_op jit(solution)/shard_map/all_to_all | solution.py:127
  78.2 14.5 %all-to-all-start.3 = ((bf16[8,1,32,256]{3,0,1,2:T(8,128)(2,1)}), bf16[8,1,32,256]{3,0,1,2:T(8,128)(2,1)S(1)}, u32[]{:S(2)}, u32[]{:S(2)}) async-start(bf16[8,1,32,256]{3,0,1,2:T(8,128)(2,1)} %get-tuple-element.22), calls=%async_computation.3 | async-start | bytes 262144 | tf_op jit(solution)/shard_map/all_to_all | solution.py:118
  83.7 1350.6 %all-reduce.13.cloned.1.call-start = ((), (), s32[]{:S(2)}) async-start(), calls=%async_computation.4 | async-start | bytes 1048576
  93.6 0.9 copy-start.2
  94.7 28.4 %collective-permute-start = (bf16[1,1,1,16,16,256]{5,4,3,2,1,0:T(8,128)(2,1)S(1)}, bf16[1,1,1,16,16,256]{5,4,3,2,1,0:T(8,128)(2,1)S(1)}, u32[]{:S(2)}, u32[]{:S(2)}) collective-permute-start(bf16[1,1,1,16,16,256]{5,4,3,2,1,0:T(8,128)(2,1)S(1)} %bitcast.713), channel_id=1, source_target_pairs={{32,0},{64,32},{96,64},{33,1},{65,33},{97,65},{34,2},{66,34},{98,6... | collective-permute-start | bytes 393224 | tf_op jit(solution)/shard_map/ppermute | solution.py:10
Sparse Core Ops, SparseCore 0:
  93.7 1340.5 all-reduce.12
where the time goes:
time: 1440 us
  waiting for transfers between devices  1330 us (92%)
  starting transfers between devices  30.1 us (2%)
  blocking collectives  27.1 us (2%)
  matrix products  23.8 us (2%)
  between operations  15.5 us (1%)
    unnamed x2, waiting for transfers between devices  1310 us
  transfers between devices with their start and end apart: 6, of which 5 were waited for; matrix products, arithmetic and copies ran while one was open for 1% of the time, Pallas kernels for 0%

commit v1 on v0

v1 whole, which is shorter than its diff:
```python
import functools

import jax
import jax.numpy as jnp
from jax import lax
from jax.experimental import pallas as pl
from jax.experimental.pallas import tpu as pltpu
from jax.sharding import PartitionSpec as P

F32 = jnp.float32
BF16 = jnp.bfloat16

C = 256
GW = 8
SIDE = 16
CELLS = SIDE * SIDE
TAPS = 27
PAD_ROWS = CELLS + 2 * SIDE
NDEV = 128
INTERPRET = False

NT = (((1,), (1,)), ((), ()))


def dot(a, b):
    return jnp.dot(a, b, preferred_element_type=F32)


def dot_nt(a, b):
    return lax.dot_general(a, b, NT, preferred_element_type=F32)


def sigmoid(v):
    return 1.0 / (1.0 + jnp.exp(-v))


def column():
    return lax.broadcasted_iota(jnp.int32, (CELLS, C), 0) % SIDE


def fill(buf, plane, sign):
    zeros = jnp.zeros((SIDE, 3 * C), BF16)
    buf[0:SIDE, :] = zeros
    buf[SIDE + CELLS :, :] = zeros
    col = column()
    ahead = jnp.where(col < SIDE - 1, pltpu.roll(plane, CELLS - 1, 0), 0.0)
    behind = jnp.where(col > 0, pltpu.roll(plane, 1, 0), 0.0)
    left, right = (behind, ahead) if sign > 0 else (ahead, behind)
    buf[SIDE : SIDE + CELLS, 0:C] = left.astype(BF16)
    buf[SIDE : SIDE + CELLS, C : 2 * C] = plane.astype(BF16)
    buf[SIDE : SIDE + CELLS, 2 * C :] = right.astype(BF16)


def conv_plane(buf, wd, depth):
    total = None
    for row in range(3):
        start = (depth * 3 + row) * 3 * C
        term = dot(buf[row * SIDE : row * SIDE + CELLS, :], wd[start : start + 3 * C, :])
        total = term if total is None else total + term
    return total


def conv_plane_back(buf, wd, depth):
    total = None
    for row in range(3):
        for col in range(3):
            start = ((depth * 3 + row) * 3 + col) * C
            rows = (2 - row) * SIDE
            term = dot_nt(
                buf[rows : rows + CELLS, col * C : (col + 1) * C], wd[start : start + C, :]
            )
            total = term if total is None else total + term
    return total


def own_kernel(x, cot, w_in, w_out, wg, slope1, h1, dh2, wd, xt, z2p, buf):
    z1 = dot(x[...], w_in[...])
    sig = sigmoid(z1)
    slope1[...] = sig * (1.0 + z1 * (1.0 - sig))
    act = (z1 * sig).astype(BF16)
    h1[...] = act
    dh2[...] = dot_nt(cot[...], w_out[...]).astype(BF16)
    same = (
        lax.broadcasted_iota(jnp.int32, (C, C), 0) // GW
        == lax.broadcasted_iota(jnp.int32, (C, C), 1) // GW
    )
    taps = wg[...].astype(F32)
    for k in range(TAPS):
        rows = jnp.broadcast_to(taps[k * GW : (k + 1) * GW, :][None], (C // GW, GW, C))
        wd[k * C : (k + 1) * C, :] = jnp.where(same, rows.reshape(C, C), 0.0).astype(BF16)
    fill(buf, act.astype(F32), 1)
    z2p[...] = conv_plane(buf, wd, 1)
    xt[...] = x[...].T


def middle_kernel(xl, xr, w_in, wd, z2p, dh2, h1l, h1r, h2, dz2, bufl, bufr):
    total = z2p[...]
    for x, h1, buf, depth in ((xl, h1l, bufl, 0), (xr, h1r, bufr, 2)):
        z1 = dot(x[...], w_in[...])
        act = (z1 * sigmoid(z1)).astype(BF16)
        h1[...] = act
        fill(buf, act.astype(F32), 1)
        total = total + conv_plane(buf, wd, depth)
    sig = sigmoid(total)
    h2[...] = (total * sig).astype(BF16)
    slope = sig * (1.0 + total * (1.0 - sig))
    dz2[...] = (dh2[...].astype(F32) * slope).astype(BF16)


def grads_kernel(h1l, h1, h1r, h2, cot, dz2, wd, grad_out, gg, dh1p, buf, ht, taps):
    fill(buf, dz2[...].astype(F32), -1)
    dh1p[...] = conv_plane_back(buf, wd, 1)
    half = C // 2
    outer = dot(h2[...].T, cot[...])
    for side in range(2):
        grad_out[side] = outer[:, side * half : (side + 1) * half]
    for depth, plane in enumerate((h1l, h1, h1r)):
        turned = plane[...].T
        for side in range(2):
            ht[side, depth * half : (depth + 1) * half, :] = turned[
                side * half : (side + 1) * half, :
            ]
    groups = half // GW
    same = (
        lax.broadcasted_iota(jnp.int32, (half, half), 0) // GW
        == lax.broadcasted_iota(jnp.int32, (half, half), 1) // GW
    )
    taps[...] = jnp.zeros_like(taps)
    for row in range(3):
        for col in range(3):
            rows = (2 - row) * SIDE
            for side in range(2):
                lanes = col * C + side * half
                full = dot(ht[side], buf[rows : rows + CELLS, lanes : lanes + half])
                for depth in range(3):
                    block = jnp.where(same, full[depth * half : (depth + 1) * half, :], 0.0)
                    k = (depth * 3 + row) * 3 + col
                    taps[k * GW : (k + 1) * GW, side * half : (side + 1) * half] = jnp.sum(
                        block.reshape(groups, GW, half), axis=0
                    )
    gg[...] = taps[...].T.reshape(C // GW, GW, C).astype(BF16)


def final_kernel(dz2l, dz2r, dh1p, wd, slope1, xt, grad_out, gg, dz1, pay, bufl, bufr, grad, pack):
    fill(bufl, dz2l[...].astype(F32), -1)
    fill(bufr, dz2r[...].astype(F32), -1)
    total = dh1p[...] + conv_plane_back(bufl, wd, 2) + conv_plane_back(bufr, wd, 0)
    back = (total.astype(BF16).astype(F32) * slope1[...]).astype(BF16)
    dz1[...] = back
    half = C // 2
    outer = dot(xt[...], back)
    for side in range(2):
        grad[side] = outer[:, side * half : (side + 1) * half]
    for which, source in enumerate((grad, grad_out)):
        for parity in range(2):
            for side in range(2):
                pack[pl.ds(which * 4 + parity * 2 + side, NDEV, stride=8), :] = source.at[
                    side
                ][pl.ds(parity, NDEV, stride=2), :]
    pay[:, :, 0:half] = pack[...].reshape(NDEV, 8, half).astype(BF16)
    blocks = C // GW
    for start in range(0, NDEV, blocks):
        pay[start : start + blocks, :, half:] = gg[...]


def dx_kernel(cot, dz1, w_in, dx):
    dx[...] = (cot[...].astype(F32) + dot_nt(dz1[...], w_in[...])).astype(BF16)


def sum_kernel(got, grad_in, grad_out, gg):
    total = jnp.sum(got[...].astype(F32), axis=0)
    half = C // 2
    for which, out in enumerate((grad_in, grad_out)):
        for parity in range(2):
            for side in range(2):
                row = which * 4 + parity * 2 + side
                out[parity : parity + 1, side * half : (side + 1) * half] = total[
                    row : row + 1, 0:half
                ]
    gg[...] = total[:, half:].T[0 : TAPS * GW, :]


def call(kernel, outs, scratch, flops, *args):
    shapes = [jax.ShapeDtypeStruct(shape, dtype) for shape, dtype in outs]
    size = sum(a.size * a.dtype.itemsize for a in (*args, *shapes))
    return pl.pallas_call(
        kernel,
        out_shape=shapes,
        in_specs=[pl.BlockSpec(memory_space=pltpu.VMEM)] * len(args),
        out_specs=[pl.BlockSpec(memory_space=pltpu.VMEM)] * len(outs),
        scratch_shapes=[pltpu.VMEM(shape, dtype) for shape, dtype in scratch],
        cost_estimate=pl.CostEstimate(flops=flops, bytes_accessed=size, transcendentals=0),
        compiler_params=pltpu.CompilerParams(vmem_limit_bytes=40 * 1024 * 1024),
        interpret=INTERPRET,
    )(*args)


PLANE = (CELLS, C)
BUF = ((PAD_ROWS, 3 * C), BF16)
TILE = 2 * C**3


def own_stage(x, cot, w_in, w_out, wg):
    return call(
        own_kernel,
        [(PLANE, F32), (PLANE, BF16), (PLANE, BF16), ((TAPS * C, C), BF16), (PLANE, BF16), (PLANE, F32)],
        [BUF],
        11 * TILE,
        x, cot, w_in, w_out, wg,
    )


def middle_stage(*args):
    return call(middle_kernel, [(PLANE, BF16)] * 4, [BUF, BUF], 20 * TILE, *args)


def grads_stage(*args):
    return call(
        grads_kernel,
        [((2, C, C // 2), F32), ((C // GW, GW, C), BF16), (PLANE, F32)],
        [BUF, ((2, 3 * C // 2, CELLS), BF16), ((C, C), F32)],
        37 * TILE,
        *args,
    )


def final_stage(*args):
    return call(
        final_kernel,
        [(PLANE, BF16), ((NDEV, 8, 3 * C // 2), BF16)],
        [BUF, BUF, ((2, C, C // 2), F32), ((NDEV * 8, C // 2), F32)],
        19 * TILE,
        *args,
    )


def dx_stage(*args):
    return call(dx_kernel, [(PLANE, BF16)], [], TILE, *args)[0]


def sum_stage(got):
    return call(sum_kernel, [((2, C), F32), ((2, C), F32), ((TAPS * GW, GW), F32)], [], 1000, got)


def shifted(value, axis, steps):
    count = lax.axis_size(axis)
    first, last = (max(0, -steps), min(count, count - steps))
    return lax.ppermute(value, axis, [(source, source + steps) for source in range(first, last)])


def per_device(inputs, cotangent, w_in, w_out, w_group):
    shape = inputs.shape
    x = inputs.reshape(PLANE)
    cot = cotangent.reshape(PLANE)
    w_in = w_in.reshape(C, C)
    w_out = w_out.reshape(C, C)
    wg = w_group.reshape(TAPS * GW, C)
    xl = shifted(x, "sg", 1)
    xr = shifted(x, "sg", -1)
    slope1, h1, dh2, wd, xt, z2p = own_stage(x, cot, w_in, w_out, wg)
    h1l, h1r, h2, dz2 = middle_stage(xl, xr, w_in, wd, z2p, dh2)
    dz2l = shifted(dz2, "sg", 1)
    dz2r = shifted(dz2, "sg", -1)
    grad_out, gg, dh1p = grads_stage(h1l, h1, h1r, h2, cot, dz2, wd)
    dz1, pay = final_stage(dz2l, dz2r, dh1p, wd, slope1, xt, grad_out, gg)
    got = lax.all_to_all(pay, ("dp", "sg"), 0, 0, tiled=True)
    dx = dx_stage(cot, dz1, w_in)
    section_grad = shifted(dx.reshape(shape), "pipe", -1)
    grad_in, grad_out, gg = sum_stage(got)
    return (
        section_grad,
        grad_in[None],
        grad_out[None],
        gg.reshape(1, 3, 3, 3, GW, GW),
    )


def solution(mesh):
    placed = (
        P("pipe", "dp", "sg", None, None, None),
        P("pipe", "dp", "sg", None, None, None),
        P("pipe", None, None),
        P("pipe", None, None),
        P("pipe", None, None, None, None, None),
    )
    return jax.shard_map(
        per_device,
        mesh=mesh,
        in_specs=placed,
        out_specs=(
            P("pipe", "dp", "sg", None, None, None),
            P("pipe", ("dp", "sg"), None),
            P("pipe", ("dp", "sg"), None),
            P("pipe", None, None, None, None, "sg"),
        ),
        check_vma=False,
    )
```

time: 1440 us -> 78.4 us (0.05)
  the two profiles are of different devices: /device:TPU:2 before, /device:TPU:8 now
where the time goes in v1:
time: 78.4 us; the launch traced here: 78.1 us
  starting transfers between devices  33.9 us (43%)
  waiting for transfers between devices  30.7 us (39%)
  Pallas kernels  7.59 us (10%)
  local copies, waits for them, and re-layouts  5.17 us (7%)
    all_to_all x1, waiting for transfers between devices, per_device(): got = lax.all_to_all(pay, ('dp', 'sg'), 0, 0, tiled=True)  21.6 us
    all_to_all x1, starting transfers between devices, per_device(): got = lax.all_to_all(pay, ('dp', 'sg'), 0, 0, tiled=True)  19.8 us
    ppermute x5, starting transfers between devices, shifted(): lax.ppermute(value, axis, [(source, source + steps) for source in range(f...  14.1 us
    ppermute x5, waiting for transfers between devices, shifted(): lax.ppermute(value, axis, [(source, source + steps) for source in range(f...  9.03 us
    pallas_call x6, Pallas kernels, call(): pl.pallas_call(kernel, out_shape=shapes, in_specs=[pl.BlockSpec(memory_sp...  7.59 us
    unnamed x15, local copies, waits for them, and re-layouts  5.17 us
  transfers between devices with their start and end apart: 6, of which 4 were waited for; matrix products, arithmetic and copies ran while one was open for 0% of the time, Pallas kernels for 4%

profile of v1, /device:TPU:8, one launch (start us, length us, event | category | flops | bytes accessed | tf_op | source)
XLA Modules:
  0.0 78.1 jit_solution(11075406904594370081)
XLA Ops:
  0.6 4.6 %collective-permute-start.1 = (bf16[256,256]{1,0:T(8,128)(2,1)}, bf16[256,256]{1,0:T(8,128)(2,1)S(1)}, u32[]{:S(2)}, u32[]{:S(2)}) collective-permute-start(bf16[256,256]{1,0:T(8,128)(2,1)} %bitcast.17), channel_id=1, source_target_pairs={{1,0},{2,1},{3,2},{4,3},{5,4},{6,5},{7,6},{8,7},{9,8},{10,9},{11,1... | collective-permute-start | bytes 393224 | tf_op jit(solution)/shard_map/ppermute | solution.py:248
  5.2 1.9 %collective-permute-start = (bf16[256,256]{1,0:T(8,128)(2,1)}, bf16[256,256]{1,0:T(8,128)(2,1)S(1)}, u32[]{:S(2)}, u32[]{:S(2)}) collective-permute-start(bf16[256,256]{1,0:T(8,128)(2,1)} %bitcast.18), channel_id=1, source_target_pairs={{0,1},{1,2},{2,3},{3,4},{4,5},{5,6},{6,7},{7,8},{8,9},{9,10},{10,1... | collective-permute-start | bytes 393224 | tf_op jit(solution)/shard_map/ppermute | solution.py:248
  7.1 0.0 copy-start
  7.1 0.9 %copy-done = bf16[1,256,256]{2,1,0:T(8,128)(2,1)S(1)} copy-done((bf16[1,256,256]{2,1,0:T(8,128)(2,1)S(1)}, bf16[1,256,256]{2,1,0:T(8,128)(2,1)}, u32[]{:S(2)}) %copy-start) | copy-done | bytes 131096
  8.0 0.0 copy-start.2
  8.0 0.9 %copy-done.2 = bf16[1,1,1,16,16,256]{5,4,3,2,1,0:T(8,128)(2,1)S(1)} copy-done((bf16[1,1,1,16,16,256]{5,4,3,2,1,0:T(8,128)(2,1)S(1)}, bf16[1,1,1,16,16,256]{5,4,3,2,1,0:T(8,128)(2,1)}, u32[]{:S(2)}) %copy-start.2) | copy-done | bytes 131096
  8.9 0.0 copy-start.4
  8.9 0.9 %copy-done.4 = bf16[1,256,256]{2,1,0:T(8,128)(2,1)S(1)} copy-done((bf16[1,256,256]{2,1,0:T(8,128)(2,1)S(1)}, bf16[1,256,256]{2,1,0:T(8,128)(2,1)}, u32[]{:S(2)}) %copy-start.4) | copy-done | bytes 131096
  9.8 0.0 copy-start.5
  9.8 0.9 %copy-done.5 = bf16[1,1,1,16,16,256]{5,4,3,2,1,0:T(8,128)(2,1)S(1)} copy-done((bf16[1,1,1,16,16,256]{5,4,3,2,1,0:T(8,128)(2,1)S(1)}, bf16[1,1,1,16,16,256]{5,4,3,2,1,0:T(8,128)(2,1)}, u32[]{:S(2)}) %copy-start.5) | copy-done | bytes 131096
  10.7 0.0 copy-start.6
  10.7 0.9 %copy-done.6 = bf16[1,3,3,3,8,256]{5,4,3,2,1,0:T(8,128)(2,1)S(1)} copy-done((bf16[1,3,3,3,8,256]{5,4,3,2,1,0:T(8,128)(2,1)S(1)}, bf16[1,3,3,3,8,256]{5,4,3,2,1,0:T(8,128)(2,1)}, u32[]{:S(2)}) %copy-start.6) | copy-done | bytes 110616
  11.6 0.0 copy-start.3
  11.6 1.1 %shard_map.84 = (f32[256,256]{1,0:T(8,128)S(1)}, bf16[256,256]{1,0:T(8,128)(2,1)S(1)}, bf16[256,256]{1,0:T(8,128)(2,1)S(1)}, bf16[6912,256]{1,0:T(8,128)(2,1)S(1...) custom-call(bf16[256,256]{1,0:T(8,128)(2,1)S(1)} %bitcast.19, bf16[256,256]{1,0:T(8,128)(2,1)S(1)} %bitcast.12, ...), custom_call_target="tpu_custom_call" | custom-call | flops 369098752 | bytes 5091328 | tf_op jit(solution)/shard_map/pallas_call | solution.py:186
  12.7 0.0 collective-permute-done.1.xr
  12.8 1.6 %collective-permute-done.xl = bf16[256,256]{1,0:T(8,128)(2,1)S(1)} collective-permute-done((bf16[256,256]{1,0:T(8,128)(2,1)}, bf16[256,256]{1,0:T(8,128)(2,1)S(1)}, u32[]{:S(2)}, u32[]{:S(2)}) %collective-permute-start) | collective-permute-done | bytes 131104 | tf_op jit(solution)/shard_map/ppermute | solution.py:248
  14.4 1.8 %shard_map.85 = (bf16[256,256]{1,0:T(8,128)(2,1)S(1)}, bf16[256,256]{1,0:T(8,128)(2,1)S(1)}, bf16[256,256]{1,0:T(8,128)(2,1)S(1)}, bf16[256,256]{1,0:T(8,128)(2,1)S(1)}) custom-call(bf16[256,256]{1,0:T(8,128)(2,1)S(1)} %collective-permute-done.xl, bf16[256,256]{1,0:T(8,128)(2,1)S(1)} %collective-permute-done.1.xr, bf16[256,256]{1,0:T(8,128)(2,1)S(1)} %bitcast.10, ...), custom_call_target="tpu_custom_call" | custom-call | flops 671088640 | bytes 4849664 | tf_op jit(solution)/shard_map/pallas_call | solution.py:186
  16.2 4.4 %collective-permute-start.3 = (bf16[256,256]{1,0:T(8,128)(2,1)S(1)}, bf16[256,256]{1,0:T(8,128)(2,1)S(1)}, u32[]{:S(2)}, u32[]{:S(2)}) collective-permute-start(bf16[256,256]{1,0:T(8,128)(2,1)S(1)} %get-tuple-element.25.dz2), channel_id=1, source_target_pairs={{1,0},{2,1},{3,2},{4,3},{5,4},{6,5},{7,6},{8,7},{9,8},{10,9},{11,1... | collective-permute-start | bytes 393224 | tf_op jit(solution)/shard_map/ppermute | solution.py:248
  20.6 1.9 %collective-permute-start.2 = (bf16[256,256]{1,0:T(8,128)(2,1)S(1)}, bf16[256,256]{1,0:T(8,128)(2,1)S(1)}, u32[]{:S(2)}, u32[]{:S(2)}) collective-permute-start(bf16[256,256]{1,0:T(8,128)(2,1)S(1)} %get-tuple-element.25.dz2), channel_id=1, source_target_pairs={{0,1},{1,2},{2,3},{3,4},{4,5},{5,6},{6,7},{7,8},{8,9},{9,10},{10,1... | collective-permute-start | bytes 393224 | tf_op jit(solution)/shard_map/ppermute | solution.py:248
  22.5 0.0 copy-done.3
  22.5 1.5 %shard_map.86 = (f32[2,256,128]{2,1,0:T(8,128)S(1)}, bf16[32,8,256]{2,1,0:T(8,128)(2,1)S(1)}, f32[256,256]{1,0:T(8,128)S(1)}) custom-call(bf16[256,256]{1,0:T(8,128)(2,1)S(1)} %get-tuple-element.26.h1l, bf16[256,256]{1,0:T(8,128)(2,1)S(1)} %get-tuple-element.27.h1, bf16[256,256]{1,0:T(8,128)(2,1)S(1)} %get-tuple-element.28.h1r, ...), custom_call_target="tpu_custom_call" | custom-call | flops 1241513984 | bytes 4980736 | tf_op jit(solution)/shard_map/pallas_call | solution.py:186
  24.1 0.0 copy-start.1
  24.1 0.0 collective-permute-done.3.dz2r
  24.1 5.5 %collective-permute-done.2.dz2l = bf16[256,256]{1,0:T(8,128)(2,1)S(1)} collective-permute-done((bf16[256,256]{1,0:T(8,128)(2,1)S(1)}, bf16[256,256]{1,0:T(8,128)(2,1)S(1)}, u32[]{:S(2)}, u32[]{:S(2)}) %collective-permute-start.2) | collective-permute-done | bytes 131104 | tf_op jit(solution)/shard_map/ppermute | solution.py:248
  29.6 2.0 %shard_map.87 = (bf16[256,256]{1,0:T(8,128)(2,1)S(1)}, bf16[128,8,384]{2,1,0:T(8,128)(2,1)}) custom-call(bf16[256,256]{1,0:T(8,128)(2,1)S(1)} %collective-permute-done.2.dz2l, bf16[256,256]{1,0:T(8,128)(2,1)S(1)} %collective-permute-done.3.dz2r, f32[256,256]{1,0:T(8,128)S(1)} %get-tuple-element.30.dh1p, bf16[6912,256]{1,0:T(8,128)(2,1)S(1)} %get-tuple-element.22.wd, ...), custom_call_target="tpu_custom_call" | custom-call | flops 637534208 | bytes 5767168 | tf_op jit(solution)/shard_map/pallas_call | solution.py:186
  31.6 19.8 %all-to-all-start = ((bf16[128,8,384]{2,1,0:T(8,128)(2,1)}), bf16[128,8,384]{2,1,0:T(8,128)(2,1)S(1)}, u32[]{:S(2)}, u32[]{:S(2)}) async-start(bf16[128,8,384]{2,1,0:T(8,128)(2,1)} %get-tuple-element.36), calls=%async_computation | async-start | bytes 1572864 | tf_op jit(solution)/shard_map/all_to_all | solution.py:266
  51.4 0.0 copy-done.1
  51.4 0.2 shard_map.88
  51.6 1.3 %collective-permute-start.4 = (bf16[1,1,1,16,16,256]{5,4,3,2,1,0:T(8,128)(2,1)S(1)}, bf16[1,1,1,16,16,256]{5,4,3,2,1,0:T(8,128)(2,1)S(1)}, u32[]{:S(2)}, u32[]{:S(2)}) collective-permute-start(bf16[1,1,1,16,16,256]{5,4,3,2,1,0:T(8,128)(2,1)S(1)} %bitcast.15), channel_id=1, source_target_pairs={{32,0},{64,32},{96,64},{33,1},{65,33},{97,65},{34,2},{66,34},{98,6... | collective-permute-start | bytes 393224 | tf_op jit(solution)/shard_map/ppermute | solution.py:248
  52.9 1.9 %collective-permute-done.4 = bf16[1,1,1,16,16,256]{5,4,3,2,1,0:T(8,128)(2,1)S(1)} collective-permute-done((bf16[1,1,1,16,16,256]{5,4,3,2,1,0:T(8,128)(2,1)S(1)}, bf16[1,1,1,16,16,256]{5,4,3,2,1,0:T(8,128)(2,1)S(1)}, u32[]{:S(2)}, u32[]{:S(2)}) %collective-permute-start.4) | collective-permute-done | bytes 131104 | tf_op jit(solution)/shard_map/ppermute | solution.py:248
  54.9 21.6 %all-to-all-done.got = bf16[128,8,384]{2,1,0:T(8,128)(2,1)S(1)} async-done(((bf16[128,8,384]{2,1,0:T(8,128)(2,1)}), bf16[128,8,384]{2,1,0:T(8,128)(2,1)S(1)}, u32[]{:S(2)}, u32[]{:S(2)}) %all-to-all-start) | async-done | bytes 786464 | tf_op jit(solution)/shard_map/all_to_all | solution.py:266
  76.5 0.9 %shard_map.89 = (f32[2,256]{1,0:T(2,128)}, f32[2,256]{1,0:T(2,128)}, f32[216,8]{1,0:T(8,128)}) custom-call(bf16[128,8,384]{2,1,0:T(8,128)(2,1)S(1)} %all-to-all-done.got), custom_call_target="tpu_custom_call" | custom-call | flops 1000 | bytes 797440 | tf_op jit(solution)/shard_map/pallas_call | solution.py:186
  77.4 0.7 copy.10
Async XLA Ops:
  0.6 12.1 %collective-permute-start.1 = (bf16[256,256]{1,0:T(8,128)(2,1)}, bf16[256,256]{1,0:T(8,128)(2,1)S(1)}, u32[]{:S(2)}, u32[]{:S(2)}) collective-permute-start(bf16[256,256]{1,0:T(8,128)(2,1)} %bitcast.17), channel_id=1, source_target_pairs={{1,0},{2,1},{3,2},{4,3},{5,4},{6,5},{7,6},{8,7},{9,8},{10,9},{11,1... | collective-permute-start | bytes 393224 | tf_op jit(solution)/shard_map/ppermute | solution.py:248
  5.2 9.2 %collective-permute-start = (bf16[256,256]{1,0:T(8,128)(2,1)}, bf16[256,256]{1,0:T(8,128)(2,1)S(1)}, u32[]{:S(2)}, u32[]{:S(2)}) collective-permute-start(bf16[256,256]{1,0:T(8,128)(2,1)} %bitcast.18), channel_id=1, source_target_pairs={{0,1},{1,2},{2,3},{3,4},{4,5},{5,6},{6,7},{7,8},{8,9},{9,10},{10,1... | collective-permute-start | bytes 393224 | tf_op jit(solution)/shard_map/ppermute | solution.py:248
  7.1 0.9 %copy-start = (bf16[1,256,256]{2,1,0:T(8,128)(2,1)S(1)}, bf16[1,256,256]{2,1,0:T(8,128)(2,1)}, u32[]{:S(2)}) copy-start(bf16[1,256,256]{2,1,0:T(8,128)(2,1)} %param.7) | copy-start | bytes 393220
  8.0 0.9 %copy-start.2 = (bf16[1,1,1,16,16,256]{5,4,3,2,1,0:T(8,128)(2,1)S(1)}, bf16[1,1,1,16,16,256]{5,4,3,2,1,0:T(8,128)(2,1)}, u32[]{:S(2)}) copy-start(bf16[1,1,1,16,16,256]{5,4,3,2,1,0:T(8,128)(2,1)} %param.6) | copy-start | bytes 393220
  8.9 0.9 %copy-start.4 = (bf16[1,256,256]{2,1,0:T(8,128)(2,1)S(1)}, bf16[1,256,256]{2,1,0:T(8,128)(2,1)}, u32[]{:S(2)}) copy-start(bf16[1,256,256]{2,1,0:T(8,128)(2,1)} %param.8) | copy-start | bytes 393220
  9.8 0.9 %copy-start.5 = (bf16[1,1,1,16,16,256]{5,4,3,2,1,0:T(8,128)(2,1)S(1)}, bf16[1,1,1,16,16,256]{5,4,3,2,1,0:T(8,128)(2,1)}, u32[]{:S(2)}) copy-start(bf16[1,1,1,16,16,256]{5,4,3,2,1,0:T(8,128)(2,1)} %param.5) | copy-start | bytes 393220
  10.7 0.9 %copy-start.6 = (bf16[1,3,3,3,8,256]{5,4,3,2,1,0:T(8,128)(2,1)S(1)}, bf16[1,3,3,3,8,256]{5,4,3,2,1,0:T(8,128)(2,1)}, u32[]{:S(2)}) copy-start(bf16[1,3,3,3,8,256]{5,4,3,2,1,0:T(8,128)(2,1)} %param.9) | copy-start | bytes 331780
  11.6 10.9 %copy-start.3 = (bf16[1,1,1,16,16,256]{5,4,3,2,1,0:T(8,128)(2,1)S(1)}, bf16[1,1,1,16,16,256]{5,4,3,2,1,0:T(8,128)(2,1)}, u32[]{:S(2)}) copy-start(bf16[1,1,1,16,16,256]{5,4,3,2,1,0:T(8,128)(2,1)} %param.6) | copy-start | bytes 393220
  16.2 7.9 %collective-permute-start.3 = (bf16[256,256]{1,0:T(8,128)(2,1)S(1)}, bf16[256,256]{1,0:T(8,128)(2,1)S(1)}, u32[]{:S(2)}, u32[]{:S(2)}) collective-permute-start(bf16[256,256]{1,0:T(8,128)(2,1)S(1)} %get-tuple-element.25.dz2), channel_id=1, source_target_pairs={{1,0},{2,1},{3,2},{4,3},{5,4},{6,5},{7,6},{8,7},{9,8},{10,9},{11,1... | collective-permute-start | bytes 393224 | tf_op jit(solution)/shard_map/ppermute | solution.py:248
  20.6 9.0 %collective-permute-start.2 = (bf16[256,256]{1,0:T(8,128)(2,1)S(1)}, bf16[256,256]{1,0:T(8,128)(2,1)S(1)}, u32[]{:S(2)}, u32[]{:S(2)}) collective-permute-start(bf16[256,256]{1,0:T(8,128)(2,1)S(1)} %get-tuple-element.25.dz2), channel_id=1, source_target_pairs={{0,1},{1,2},{2,3},{3,4},{4,5},{5,6},{6,7},{7,8},{8,9},{9,10},{10,1... | collective-permute-start | bytes 393224 | tf_op jit(solution)/shard_map/ppermute | solution.py:248
  24.1 27.3 %copy-start.1 = (bf16[1,256,256]{2,1,0:T(8,128)(2,1)S(1)}, bf16[1,256,256]{2,1,0:T(8,128)(2,1)}, u32[]{:S(2)}) copy-start(bf16[1,256,256]{2,1,0:T(8,128)(2,1)} %param.7) | copy-start | bytes 393220
  31.6 44.9 %all-to-all-start = ((bf16[128,8,384]{2,1,0:T(8,128)(2,1)}), bf16[128,8,384]{2,1,0:T(8,128)(2,1)S(1)}, u32[]{:S(2)}, u32[]{:S(2)}) async-start(bf16[128,8,384]{2,1,0:T(8,128)(2,1)} %get-tuple-element.36), calls=%async_computation | async-start | bytes 1572864 | tf_op jit(solution)/shard_map/all_to_all | solution.py:266
  51.6 3.2 %collective-permute-start.4 = (bf16[1,1,1,16,16,256]{5,4,3,2,1,0:T(8,128)(2,1)S(1)}, bf16[1,1,1,16,16,256]{5,4,3,2,1,0:T(8,128)(2,1)S(1)}, u32[]{:S(2)}, u32[]{:S(2)}) collective-permute-start(bf16[1,1,1,16,16,256]{5,4,3,2,1,0:T(8,128)(2,1)S(1)} %bitcast.15), channel_id=1, source_target_pairs={{32,0},{64,32},{96,64},{33,1},{65,33},{97,65},{34,2},{66,34},{98,6... | collective-permute-start | bytes 393224 | tf_op jit(solution)/shard_map/ppermute | solution.py:248

commit v2 on v1

v2 whole, which is shorter than its diff:
```python
import functools

import jax
import jax.numpy as jnp
from jax import lax
from jax.experimental import pallas as pl
from jax.experimental.pallas import tpu as pltpu
from jax.sharding import PartitionSpec as P

F32 = jnp.float32
BF16 = jnp.bfloat16

C = 256
GW = 8
SIDE = 16
CELLS = SIDE * SIDE
TAPS = 27
PAD_ROWS = CELLS + 2 * SIDE
NDEV = 128
INTERPRET = False

NT = (((1,), (1,)), ((), ()))


def dot(a, b):
    return jnp.dot(a, b, preferred_element_type=F32)


def dot_nt(a, b):
    return lax.dot_general(a, b, NT, preferred_element_type=F32)


def sigmoid(v):
    return 1.0 / (1.0 + jnp.exp(-v))


def column():
    return lax.broadcasted_iota(jnp.int32, (CELLS, C), 0) % SIDE


def fill(buf, plane, sign):
    zeros = jnp.zeros((SIDE, 3 * C), BF16)
    buf[0:SIDE, :] = zeros
    buf[SIDE + CELLS :, :] = zeros
    col = column()
    ahead = jnp.where(col < SIDE - 1, pltpu.roll(plane, CELLS - 1, 0), 0.0)
    behind = jnp.where(col > 0, pltpu.roll(plane, 1, 0), 0.0)
    left, right = (behind, ahead) if sign > 0 else (ahead, behind)
    buf[SIDE : SIDE + CELLS, 0:C] = left.astype(BF16)
    buf[SIDE : SIDE + CELLS, C : 2 * C] = plane.astype(BF16)
    buf[SIDE : SIDE + CELLS, 2 * C :] = right.astype(BF16)


def conv_plane(buf, wd, depth):
    total = None
    for row in range(3):
        start = (depth * 3 + row) * 3 * C
        term = dot(buf[row * SIDE : row * SIDE + CELLS, :], wd[start : start + 3 * C, :])
        total = term if total is None else total + term
    return total


def conv_plane_back(buf, wd, depth):
    total = None
    for row in range(3):
        for col in range(3):
            start = ((depth * 3 + row) * 3 + col) * C
            rows = (2 - row) * SIDE
            term = dot_nt(
                buf[rows : rows + CELLS, col * C : (col + 1) * C], wd[start : start + C, :]
            )
            total = term if total is None else total + term
    return total


def spread(wg, wd, which):
    same = (
        lax.broadcasted_iota(jnp.int32, (C, C), 0) // GW
        == lax.broadcasted_iota(jnp.int32, (C, C), 1) // GW
    )
    taps = wg[...].astype(F32)
    for k in which:
        rows = jnp.broadcast_to(taps[k * GW : (k + 1) * GW, :][None], (C // GW, GW, C))
        wd[k * C : (k + 1) * C, :] = jnp.where(same, rows.reshape(C, C), 0.0).astype(BF16)


def own_kernel(
    x_hbm, cot_hbm, w_in_hbm, w_out_hbm, wg_hbm,
    slope1, h1, dh2, wd, z2p, x, cot, w_in,
    buf, w_out, wg, sems,
):
    copies = [
        pltpu.make_async_copy(source, target, sems.at[i])
        for i, (source, target) in enumerate(
            ((wg_hbm, wg), (x_hbm, x), (w_in_hbm, w_in), (cot_hbm, cot), (w_out_hbm, w_out))
        )
    ]
    for copy in copies:
        copy.start()
    copies[0].wait()
    spread(wg, wd, range(TAPS))
    for copy in copies[1:]:
        copy.wait()
    z1 = dot(x[...], w_in[...])
    sig = sigmoid(z1)
    slope1[...] = sig * (1.0 + z1 * (1.0 - sig))
    act = (z1 * sig).astype(BF16)
    h1[...] = act
    dh2[...] = dot_nt(cot[...], w_out[...]).astype(BF16)
    fill(buf, act.astype(F32), 1)
    z2p[...] = conv_plane(buf, wd, 1)


def middle_kernel(
    xl, x, xr, cot, w_in, wd, z2p, dh2, h1, slope1,
    own, left, right, pay,
    bufl, bufr, buf, ht, slopes, taps, grads, pack,
):
    half = C // 2
    total = z2p[...]
    for x_next, b, depth in ((xl, bufl, 0), (xr, bufr, 2)):
        z1 = dot(x_next[...], w_in[...])
        sig = sigmoid(z1)
        slopes[depth // 2] = sig * (1.0 + z1 * (1.0 - sig))
        fill(b, (z1 * sig).astype(BF16).astype(F32), 1)
        total = total + conv_plane(b, wd, depth)
    sig = sigmoid(total)
    h2 = (total * sig).astype(BF16)
    slope = sig * (1.0 + total * (1.0 - sig))
    back = (dh2[...].astype(F32) * slope).astype(BF16)
    fill(buf, back.astype(F32), -1)
    outer = dot(h2.T, cot[...])
    for side in range(2):
        grads[2 + side] = outer[:, side * half : (side + 1) * half]
    share = (conv_plane_back(buf, wd, 1) * slope1[...]).astype(BF16)
    own[...] = share
    outer = dot(x[...].T, share)
    for x_next, out, depth in ((xl, left, 0), (xr, right, 2)):
        share = (conv_plane_back(buf, wd, depth) * slopes[depth // 2]).astype(BF16)
        outer = outer + dot(x_next[...].T, share)
        out[...] = share
    for side in range(2):
        grads[side] = outer[:, side * half : (side + 1) * half]
    for depth, plane in enumerate((bufl, None, bufr)):
        value = h1[...] if plane is None else plane[SIDE : SIDE + CELLS, C : 2 * C]
        turned = value.T
        for side in range(2):
            ht[side, depth * half : (depth + 1) * half, :] = turned[
                side * half : (side + 1) * half, :
            ]
    groups = half // GW
    same = (
        lax.broadcasted_iota(jnp.int32, (half, half), 0) // GW
        == lax.broadcasted_iota(jnp.int32, (half, half), 1) // GW
    )
    taps[TAPS * GW :, :] = jnp.zeros((C - TAPS * GW, C), F32)
    for row in range(3):
        for col in range(3):
            rows = (2 - row) * SIDE
            for side in range(2):
                lanes = col * C + side * half
                full = dot(ht[side], buf[rows : rows + CELLS, lanes : lanes + half])
                for depth in range(3):
                    block = jnp.where(same, full[depth * half : (depth + 1) * half, :], 0.0)
                    k = (depth * 3 + row) * 3 + col
                    taps[k * GW : (k + 1) * GW, side * half : (side + 1) * half] = jnp.sum(
                        block.reshape(groups, GW, half), axis=0
                    )
    for which in range(2):
        for parity in range(2):
            for side in range(2):
                pack[pl.ds(which * 4 + parity * 2 + side, NDEV, stride=8), :] = grads.at[
                    which * 2 + side
                ][pl.ds(parity, NDEV, stride=2), :]
    blocks = C // GW
    packed = pack[...].reshape(NDEV, 8, half).astype(BF16)
    gg = taps[...].T.reshape(blocks, GW, C).astype(BF16)
    for part in range(NDEV // blocks):
        pay[:, :, part * half : (part + 1) * half] = packed[part * blocks : (part + 1) * blocks]
    pay[:, :, 4 * half :] = gg


def dx_kernel(own, left, right, cot, w_in, dx, dxl, dxr):
    dx[...] = (cot[...].astype(F32) + dot_nt(own[...], w_in[...])).astype(BF16)
    dxl[...] = dot_nt(left[...], w_in[...]).astype(BF16)
    dxr[...] = dot_nt(right[...], w_in[...]).astype(BF16)


def first_sum_kernel(got, pay):
    total = jnp.sum(got[...].astype(F32), axis=0)
    half = C // 2
    for part in range(4):
        pay[part, :, 0:half] = total[:, part * half : (part + 1) * half]
        pay[part, :, half:] = total[:, 4 * half :]


def sum_kernel(got, dx, dxl, dxr, grad_in, grad_out, gg, section):
    section[...] = (
        dx[...].astype(F32) + (dxl[...].astype(F32) + dxr[...].astype(F32))
    ).astype(BF16)
    total = jnp.sum(got[...].astype(F32), axis=0)
    half = C // 2
    for which, out in enumerate((grad_in, grad_out)):
        for parity in range(2):
            for side in range(2):
                row = which * 4 + parity * 2 + side
                out[parity : parity + 1, side * half : (side + 1) * half] = total[
                    row : row + 1, 0:half
                ]
    gg[...] = total[:, half:].T[0 : TAPS * GW, :]


def call(kernel, outs, scratch, flops, *args, space=pltpu.VMEM):
    shapes = [jax.ShapeDtypeStruct(shape, dtype) for shape, dtype in outs]
    size = sum(a.size * a.dtype.itemsize for a in (*args, *shapes))
    return pl.pallas_call(
        kernel,
        out_shape=shapes,
        in_specs=[pl.BlockSpec(memory_space=space)] * len(args),
        out_specs=[pl.BlockSpec(memory_space=pltpu.VMEM)] * len(outs),
        scratch_shapes=[
            pltpu.VMEM(*entry) if isinstance(entry, tuple) else entry for entry in scratch
        ],
        cost_estimate=pl.CostEstimate(flops=flops, bytes_accessed=size, transcendentals=0),
        compiler_params=pltpu.CompilerParams(vmem_limit_bytes=8 * 1024 * 1024),
        interpret=INTERPRET,
    )(*args)


PLANE = (CELLS, C)
BUF = ((PAD_ROWS, 3 * C), BF16)
PAY = (C // GW, 8, 3 * C)
TILE = 2 * C**3


def own_stage(x, cot, w_in, w_out, wg):
    return call(
        own_kernel,
        [(PLANE, F32), (PLANE, BF16), (PLANE, BF16), ((TAPS * C, C), BF16), (PLANE, F32)]
        + [(PLANE, BF16)] * 3,
        [BUF, (PLANE, BF16), ((TAPS * GW, C), BF16), pltpu.SemaphoreType.DMA((5,))],
        11 * TILE,
        x, cot, w_in, w_out, wg,
        space=pltpu.HBM,
    )


def middle_stage(*args):
    return call(
        middle_kernel,
        [(PLANE, BF16)] * 3 + [(PAY, BF16)],
        [
            BUF, BUF, BUF,
            ((2, 3 * C // 2, CELLS), BF16),
            ((2, CELLS, C), F32),
            ((C, C), F32),
            ((4, C, C // 2), F32),
            ((NDEV * 8, C // 2), F32),
        ],
        80 * TILE,
        *args,
    )


def dx_stage(*args):
    return call(dx_kernel, [(PLANE, BF16)] * 3, [], 3 * TILE, *args)


def first_sum_stage(got):
    return call(first_sum_kernel, [((4, 8, 3 * C // 2), F32)], [], 1000, got)[0]


def sum_stage(*args):
    return call(
        sum_kernel,
        [((2, C), F32), ((2, C), F32), ((TAPS * GW, GW), F32), (PLANE, BF16)],
        [],
        1000,
        *args,
    )


def shifted(value, steps):
    pipes, planes = lax.axis_size("pipe"), lax.axis_size("sg")
    pairs = [
        (pipe * planes + plane, (pipe + steps[0]) * planes + plane + steps[1])
        for pipe in range(pipes)
        for plane in range(planes)
        if 0 <= pipe + steps[0] < pipes and 0 <= plane + steps[1] < planes
    ]
    return lax.ppermute(value, ("pipe", "sg"), pairs)


def per_device(inputs, cotangent, w_in, w_out, w_group):
    shape = inputs.shape
    x = inputs.reshape(PLANE)
    cot = cotangent.reshape(PLANE)
    w_in = w_in.reshape(C, C)
    w_out = w_out.reshape(C, C)
    wg = w_group.reshape(TAPS * GW, C)
    xl = shifted(x, (0, 1))
    xr = shifted(x, (0, -1))
    kept = [
        pltpu.with_memory_space_constraint(value, pltpu.HBM)
        for value in (x, cot, w_in, w_out, wg)
    ]
    slope1, h1, dh2, wd, z2p, x, cot, w_in = own_stage(*kept)
    own, left, right, pay = middle_stage(xl, x, xr, cot, w_in, wd, z2p, dh2, h1, slope1)
    dx, dxl, dxr = dx_stage(own, left, right, cot, w_in)
    part = first_sum_stage(lax.all_to_all(pay, "sg", 0, 0, tiled=True))
    got = lax.all_to_all(part, "dp", 0, 0, tiled=True)
    grad_in, grad_out, gg, section_grad = sum_stage(
        got, shifted(dx, (-1, 0)), shifted(dxl, (-1, -1)), shifted(dxr, (-1, 1))
    )
    return (
        section_grad.reshape(shape),
        grad_in[None],
        grad_out[None],
        gg.reshape(1, 3, 3, 3, GW, GW),
    )


def solution(mesh):
    placed = (
        P("pipe", "dp", "sg", None, None, None),
        P("pipe", "dp", "sg", None, None, None),
        P("pipe", None, None),
        P("pipe", None, None),
        P("pipe", None, None, None, None, None),
    )
    return jax.shard_map(
        per_device,
        mesh=mesh,
        in_specs=placed,
        out_specs=(
            P("pipe", "dp", "sg", None, None, None),
            P("pipe", ("dp", "sg"), None),
            P("pipe", ("dp", "sg"), None),
            P("pipe", None, None, None, None, "sg"),
        ),
        check_vma=False,
    )
```

time: 78.4 us -> 62.8 us (0.80)
  waiting for transfers between devices: 30.7 us -> 22.3 us
  local copies, waits for them, and re-layouts: 5.17 us -> 0 us
  starting transfers between devices: 33.9 us -> 29.6 us
  Pallas kernels: 7.59 us -> 9.73 us
    unnamed x15 -> x0, local copies, waits for them, and re-layouts: 5.17 us -> none
    all_to_all x1 -> x2, waiting for transfers between devices: 21.6 us -> 17.3 us  [the longest x1 9.13 us: per_device(): part = first_sum_stage(lax.all_to_all(pay, 'sg', 0, 0, tiled=True))]
    ppermute x5, waiting for transfers between devices: 9.03 us -> 5.03 us  [shifted(): return lax.ppermute(value, ('pipe', 'sg'), pairs)]
    ppermute x5, starting transfers between devices: 14.1 us -> 10.3 us  [shifted(): return lax.ppermute(value, ('pipe', 'sg'), pairs)]
    pallas_call x6 -> x5, Pallas kernels: 7.59 us -> 9.73 us  [call(): pl.pallas_call(kernel, out_shape=shapes, in_specs=[pl.BlockSpec(memory_sp...]
    all_to_all x1 -> x2, starting transfers between devices: 19.8 us -> 19.2 us  [the longest x1 10.3 us: per_device(): got = lax.all_to_all(part, 'dp', 0, 0, tiled=True)]
  transfers between devices with their start and end apart: 6 -> 7, of which waited for: 4 -> 3; matrix products, arithmetic and copies ran while one was open for 0% -> 0% of each run, Pallas kernels for 4% -> 5%
where the time goes in v2:
time: 62.8 us; the launch traced here: 62.3 us
  starting transfers between devices  29.6 us (47%)
  waiting for transfers between devices  22.3 us (36%)
  Pallas kernels  9.73 us (15%)
  between operations  0.72 us (1%)
    ppermute x5, starting transfers between devices, shifted(): return lax.ppermute(value, ('pipe', 'sg'), pairs)  10.3 us
    all_to_all x1, starting transfers between devices, per_device(): got = lax.all_to_all(part, 'dp', 0, 0, tiled=True)  10.3 us
    pallas_call x5, Pallas kernels, call(): pl.pallas_call(kernel, out_shape=shapes, in_specs=[pl.BlockSpec(memory_sp...  9.73 us
    all_to_all x1, waiting for transfers between devices, per_device(): part = first_sum_stage(lax.all_to_all(pay, 'sg', 0, 0, tiled=True))  9.13 us
    all_to_all x1, starting transfers between devices, per_device(): part = first_sum_stage(lax.all_to_all(pay, 'sg', 0, 0, tiled=True))  8.92 us
    all_to_all x1, waiting for transfers between devices, per_device(): got = lax.all_to_all(part, 'dp', 0, 0, tiled=True)  8.16 us
    ppermute x5, waiting for transfers between devices, shifted(): return lax.ppermute(value, ('pipe', 'sg'), pairs)  5.03 us
  transfers between devices with their start and end apart: 7, of which 3 were waited for; matrix products, arithmetic and copies ran while one was open for 0% of the time, Pallas kernels for 5%

profile of v2, /device:TPU:8, one launch (start us, length us, event | category | flops | bytes accessed | tf_op | source)
XLA Modules:
  0.0 62.3 jit_solution(17846462955802786718)
XLA Ops:
  0.6 4.6 %collective-permute-start.1 = (bf16[256,256]{1,0:T(8,128)(2,1)}, bf16[256,256]{1,0:T(8,128)(2,1)S(1)}, u32[]{:S(2)}, u32[]{:S(2)}) collective-permute-start(bf16[256,256]{1,0:T(8,128)(2,1)} %bitcast.12), channel_id=1, source_target_pairs={{1,0},{2,1},{3,2},{4,3},{5,4},{6,5},{7,6},{8,7},{9,8},{10,9},{11,1... | collective-permute-start | bytes 393224 | tf_op jit(solution)/shard_map/ppermute | solution.py:291
  5.2 1.9 %collective-permute-start = (bf16[256,256]{1,0:T(8,128)(2,1)}, bf16[256,256]{1,0:T(8,128)(2,1)S(1)}, u32[]{:S(2)}, u32[]{:S(2)}) collective-permute-start(bf16[256,256]{1,0:T(8,128)(2,1)} %bitcast.13), channel_id=1, source_target_pairs={{0,1},{1,2},{2,3},{3,4},{4,5},{5,6},{6,7},{7,8},{8,9},{9,10},{10,1... | collective-permute-start | bytes 393224 | tf_op jit(solution)/shard_map/ppermute | solution.py:291
  7.1 2.2 %shard_map.84 = (f32[256,256]{1,0:T(8,128)S(1)}, bf16[256,256]{1,0:T(8,128)(2,1)S(1)}, bf16[256,256]{1,0:T(8,128)(2,1)S(1)}, bf16[6912,256]{1,0:T(8,128)(2,1)S(1...) custom-call(bf16[256,256]{1,0:T(8,128)(2,1)} %bitcast.14, ...), custom_call_target="tpu_custom_call" | custom-call | flops 369098752 | bytes 5353472 | tf_op jit(solution)/shard_map/pallas_call | solution.py:216
  9.3 0.0 collective-permute-done.1.xr
  9.4 5.0 %collective-permute-done.xl = bf16[256,256]{1,0:T(8,128)(2,1)S(1)} collective-permute-done((bf16[256,256]{1,0:T(8,128)(2,1)}, bf16[256,256]{1,0:T(8,128)(2,1)S(1)}, u32[]{:S(2)}, u32[]{:S(2)}) %collective-permute-start) | collective-permute-done | bytes 131104 | tf_op jit(solution)/shard_map/ppermute | solution.py:291
  14.4 5.7 %shard_map.85 = (bf16[256,256]{1,0:T(8,128)(2,1)S(1)}, bf16[256,256]{1,0:T(8,128)(2,1)S(1)}, bf16[256,256]{1,0:T(8,128)(2,1)S(1)}, bf16[32,8,768]{2,1,0:T(8,128)(2,1)}) custom-call(bf16[256,256]{1,0:T(8,128)(2,1)S(1)} %collective-permute-done.xl, bf16[256,256]{1,0:T(8,128)(2,1)S(1)} %get-tuple-element.23.x, bf16[256,256]{1,0:T(8,128)(2,1)S(1)} %collective-permute-done.1.xr, ...), custom_call_target="tpu_custom_call" | custom-call | flops 2684354560 | bytes 5767168 | tf_op jit(solution)/shard_map/pallas_call | solution.py:216
  20.1 8.9 %all-to-all-start = ((bf16[32,8,768]{2,1,0:T(8,128)(2,1)}), bf16[32,8,768]{2,1,0:T(8,128)(2,1)S(1)}, u32[]{:S(2)}, u32[]{:S(2)}) async-start(bf16[32,8,768]{2,1,0:T(8,128)(2,1)} %get-tuple-element.31), calls=%async_computation | async-start | bytes 786432 | tf_op jit(solution)/shard_map/all_to_all | solution.py:310
  29.0 0.3 shard_map.87
  29.3 1.3 %collective-permute-start.2 = (bf16[256,256]{1,0:T(8,128)(2,1)S(1)}, bf16[256,256]{1,0:T(8,128)(2,1)S(1)}, u32[]{:S(2)}, u32[]{:S(2)}) collective-permute-start(bf16[256,256]{1,0:T(8,128)(2,1)S(1)} %get-tuple-element.35), channel_id=1, source_target_pairs={{32,0},{33,1},{34,2},{35,3},{36,4},{37,5},{38,6},{39,7},{40,8},{41... | collective-permute-start | bytes 393224 | tf_op jit(solution)/shard_map/ppermute | solution.py:291
  30.6 1.3 %collective-permute-start.3 = (bf16[256,256]{1,0:T(8,128)(2,1)S(1)}, bf16[256,256]{1,0:T(8,128)(2,1)S(1)}, u32[]{:S(2)}, u32[]{:S(2)}) collective-permute-start(bf16[256,256]{1,0:T(8,128)(2,1)S(1)} %get-tuple-element.36), channel_id=1, source_target_pairs={{33,0},{34,1},{35,2},{36,3},{37,4},{38,5},{39,6},{40,7},{41,8},{42... | collective-permute-start | bytes 393224 | tf_op jit(solution)/shard_map/ppermute | solution.py:291
  31.9 1.3 %collective-permute-start.4 = (bf16[256,256]{1,0:T(8,128)(2,1)S(1)}, bf16[256,256]{1,0:T(8,128)(2,1)S(1)}, u32[]{:S(2)}, u32[]{:S(2)}) collective-permute-start(bf16[256,256]{1,0:T(8,128)(2,1)S(1)} %get-tuple-element.37), channel_id=1, source_target_pairs={{32,1},{33,2},{34,3},{35,4},{36,5},{37,6},{38,7},{39,8},{40,9},{41... | collective-permute-start | bytes 393224 | tf_op jit(solution)/shard_map/ppermute | solution.py:291
  33.2 9.1 %all-to-all-done.got = bf16[32,8,768]{2,1,0:T(8,128)(2,1)S(1)} async-done(((bf16[32,8,768]{2,1,0:T(8,128)(2,1)}), bf16[32,8,768]{2,1,0:T(8,128)(2,1)S(1)}, u32[]{:S(2)}, u32[]{:S(2)}) %all-to-all-start) | async-done | bytes 393248 | tf_op jit(solution)/shard_map/all_to_all | solution.py:310
  42.3 0.7 %shard_map.86 = f32[4,8,384]{2,1,0:T(8,128)} custom-call(bf16[32,8,768]{2,1,0:T(8,128)(2,1)S(1)} %all-to-all-done.got), custom_call_target="tpu_custom_call" | custom-call | flops 1000 | bytes 442368 | tf_op jit(solution)/shard_map/pallas_call | solution.py:216
  43.0 10.3 %all-to-all-start.1 = ((f32[4,8,384]{2,1,0:T(8,128)}), f32[4,8,384]{2,1,0:T(8,128)S(1)}, u32[]{:S(2)}, u32[]{:S(2)}) async-start(f32[4,8,384]{2,1,0:T(8,128)} %shard_map.86), calls=%async_computation.1 | async-start | bytes 98304 | tf_op jit(solution)/shard_map/all_to_all | solution.py:311
  53.3 0.0 collective-permute-done.2.dx
  53.3 0.0 collective-permute-done.3.dxl
  53.3 0.0 collective-permute-done.4.dxr
  53.3 8.2 %all-to-all-done.1.got = f32[4,8,384]{2,1,0:T(8,128)S(1)} async-done(((f32[4,8,384]{2,1,0:T(8,128)}), f32[4,8,384]{2,1,0:T(8,128)S(1)}, u32[]{:S(2)}, u32[]{:S(2)}) %all-to-all-start.1) | async-done | bytes 49184 | tf_op jit(solution)/shard_map/all_to_all | solution.py:311
  61.5 0.8 %shard_map.88 = (f32[2,256]{1,0:T(2,128)}, f32[2,256]{1,0:T(2,128)}, f32[216,8]{1,0:T(8,128)}, bf16[256,256]{1,0:T(8,128)(2,1)}) custom-call(f32[4,8,384]{2,1,0:T(8,128)S(1)} %all-to-all-done.1.got, bf16[256,256]{1,0:T(8,128)(2,1)S(1)} %collective-permute-done.2.dx, bf16[256,256]{1,0:T(8,128)(2,1)S(1)} %collective-permute-done.3.dxl, ...), custom_call_target="tpu_custom_call" | custom-call | flops 1000 | bytes 584448 | tf_op jit(solution)/shard_map/pallas_call | solution.py:216
Async XLA Ops:
  0.6 8.7 %collective-permute-start.1 = (bf16[256,256]{1,0:T(8,128)(2,1)}, bf16[256,256]{1,0:T(8,128)(2,1)S(1)}, u32[]{:S(2)}, u32[]{:S(2)}) collective-permute-start(bf16[256,256]{1,0:T(8,128)(2,1)} %bitcast.12), channel_id=1, source_target_pairs={{1,0},{2,1},{3,2},{4,3},{5,4},{6,5},{7,6},{8,7},{9,8},{10,9},{11,1... | collective-permute-start | bytes 393224 | tf_op jit(solution)/shard_map/ppermute | solution.py:291
  5.2 9.2 %collective-permute-start = (bf16[256,256]{1,0:T(8,128)(2,1)}, bf16[256,256]{1,0:T(8,128)(2,1)S(1)}, u32[]{:S(2)}, u32[]{:S(2)}) collective-permute-start(bf16[256,256]{1,0:T(8,128)(2,1)} %bitcast.13), channel_id=1, source_target_pairs={{0,1},{1,2},{2,3},{3,4},{4,5},{5,6},{6,7},{7,8},{8,9},{9,10},{10,1... | collective-permute-start | bytes 393224 | tf_op jit(solution)/shard_map/ppermute | solution.py:291
  20.1 22.3 %all-to-all-start = ((bf16[32,8,768]{2,1,0:T(8,128)(2,1)}), bf16[32,8,768]{2,1,0:T(8,128)(2,1)S(1)}, u32[]{:S(2)}, u32[]{:S(2)}) async-start(bf16[32,8,768]{2,1,0:T(8,128)(2,1)} %get-tuple-element.31), calls=%async_computation | async-start | bytes 786432 | tf_op jit(solution)/shard_map/all_to_all | solution.py:310
  29.3 24.0 %collective-permute-start.2 = (bf16[256,256]{1,0:T(8,128)(2,1)S(1)}, bf16[256,256]{1,0:T(8,128)(2,1)S(1)}, u32[]{:S(2)}, u32[]{:S(2)}) collective-permute-start(bf16[256,256]{1,0:T(8,128)(2,1)S(1)} %get-tuple-element.35), channel_id=1, source_target_pairs={{32,0},{33,1},{34,2},{35,3},{36,4},{37,5},{38,6},{39,7},{40,8},{41... | collective-permute-start | bytes 393224 | tf_op jit(solution)/shard_map/ppermute | solution.py:291
  30.6 22.7 %collective-permute-start.3 = (bf16[256,256]{1,0:T(8,128)(2,1)S(1)}, bf16[256,256]{1,0:T(8,128)(2,1)S(1)}, u32[]{:S(2)}, u32[]{:S(2)}) collective-permute-start(bf16[256,256]{1,0:T(8,128)(2,1)S(1)} %get-tuple-element.36), channel_id=1, source_target_pairs={{33,0},{34,1},{35,2},{36,3},{37,4},{38,5},{39,6},{40,7},{41,8},{42... | collective-permute-start | bytes 393224 | tf_op jit(solution)/shard_map/ppermute | solution.py:291
  31.9 21.4 %collective-permute-start.4 = (bf16[256,256]{1,0:T(8,128)(2,1)S(1)}, bf16[256,256]{1,0:T(8,128)(2,1)S(1)}, u32[]{:S(2)}, u32[]{:S(2)}) collective-permute-start(bf16[256,256]{1,0:T(8,128)(2,1)S(1)} %get-tuple-element.37), channel_id=1, source_target_pairs={{32,1},{33,2},{34,3},{35,4},{36,5},{37,6},{38,7},{39,8},{40,9},{41... | collective-permute-start | bytes 393224 | tf_op jit(solution)/shard_map/ppermute | solution.py:291
  43.0 18.5 %all-to-all-start.1 = ((f32[4,8,384]{2,1,0:T(8,128)}), f32[4,8,384]{2,1,0:T(8,128)S(1)}, u32[]{:S(2)}, u32[]{:S(2)}) async-start(f32[4,8,384]{2,1,0:T(8,128)} %shard_map.86), calls=%async_computation.1 | async-start | bytes 98304 | tf_op jit(solution)/shard_map/all_to_all | solution.py:311

commit v3 on v2

--- a/solution.py
+++ b/solution.py
@@ -112,11 +112,25 @@
 
 
 def middle_kernel(
-    xl, x, xr, cot, w_in, wd, z2p, dh2, h1, slope1,
-    own, left, right, pay,
-    bufl, bufr, buf, ht, slopes, taps, grads, pack,
+    near, far, x, cot, w_in, wd, z2p, dh2, h1, slope1,
+    own, to_near, to_far, pay,
+    bufl, bufr, buf, ht, slopes, taps, grads, pack, xl, xr, left, right,
 ):
     half = C // 2
+    even = lax.axis_index("sg") % 2 == 0
+
+    def swap(pair, out):
+        @pl.when(even)
+        def _():
+            out[0][...] = pair[1][...]
+            out[1][...] = pair[0][...]
+
+        @pl.when(jnp.logical_not(even))
+        def _():
+            out[0][...] = pair[0][...]
+            out[1][...] = pair[1][...]
+
+    swap((near, far), (xl, xr))
     total = z2p[...]
     for x_next, b, depth in ((xl, bufl, 0), (xr, bufr, 2)):
         z1 = dot(x_next[...], w_in[...])
@@ -139,6 +153,7 @@
         share = (conv_plane_back(buf, wd, depth) * slopes[depth // 2]).astype(BF16)
         outer = outer + dot(x_next[...].T, share)
         out[...] = share
+    swap((left, right), (to_near, to_far))
     for side in range(2):
         grads[side] = outer[:, side * half : (side + 1) * half]
     for depth, plane in enumerate((bufl, None, bufr)):
@@ -180,10 +195,13 @@
     pay[:, :, 4 * half :] = gg
 
 
-def dx_kernel(own, left, right, cot, w_in, dx, dxl, dxr):
+def own_dx_kernel(own, cot, w_in, dx):
     dx[...] = (cot[...].astype(F32) + dot_nt(own[...], w_in[...])).astype(BF16)
-    dxl[...] = dot_nt(left[...], w_in[...]).astype(BF16)
-    dxr[...] = dot_nt(right[...], w_in[...]).astype(BF16)
+
+
+def pair_dx_kernel(near, far, w_in, dx_near, dx_far):
+    dx_near[...] = dot_nt(near[...], w_in[...]).astype(BF16)
+    dx_far[...] = dot_nt(far[...], w_in[...]).astype(BF16)
 
 
 def first_sum_kernel(got, pay):
@@ -256,14 +274,19 @@
             ((C, C), F32),
             ((4, C, C // 2), F32),
             ((NDEV * 8, C // 2), F32),
-        ],
+        ]
+        + [(PLANE, BF16)] * 4,
         80 * TILE,
         *args,
     )
 
 
-def dx_stage(*args):
-    return call(dx_kernel, [(PLANE, BF16)] * 3, [], 3 * TILE, *args)
+def own_dx_stage(*args):
+    return call(own_dx_kernel, [(PLANE, BF16)], [], TILE, *args)[0]
+
+
+def pair_dx_stage(*args):
+    return call(pair_dx_kernel, [(PLANE, BF16)] * 2, [], 2 * TILE, *args)
 
 
 def first_sum_stage(got):
@@ -280,13 +303,21 @@
     )
 
 
-def shifted(value, steps):
+def near_of(plane):
+    return plane ^ 1
+
+
+def far_of(plane):
+    return plane - 1 if plane % 2 == 0 else plane + 1
+
+
+def sent(value, back, partner):
     pipes, planes = lax.axis_size("pipe"), lax.axis_size("sg")
     pairs = [
-        (pipe * planes + plane, (pipe + steps[0]) * planes + plane + steps[1])
-        for pipe in range(pipes)
+        (pipe * planes + plane, (pipe - back) * planes + partner(plane))
+        for pipe in range(back, pipes)
         for plane in range(planes)
-        if 0 <= pipe + steps[0] < pipes and 0 <= plane + steps[1] < planes
+        if 0 <= partner(plane) < planes
     ]
     return lax.ppermute(value, ("pipe", "sg"), pairs)
 
@@ -298,20 +329,24 @@
     w_in = w_in.reshape(C, C)
     w_out = w_out.reshape(C, C)
     wg = w_group.reshape(TAPS * GW, C)
-    xl = shifted(x, (0, 1))
-    xr = shifted(x, (0, -1))
+    far = sent(x, 0, far_of)
+    near = sent(x, 0, near_of)
     kept = [
         pltpu.with_memory_space_constraint(value, pltpu.HBM)
         for value in (x, cot, w_in, w_out, wg)
     ]
     slope1, h1, dh2, wd, z2p, x, cot, w_in = own_stage(*kept)
-    own, left, right, pay = middle_stage(xl, x, xr, cot, w_in, wd, z2p, dh2, h1, slope1)
-    dx, dxl, dxr = dx_stage(own, left, right, cot, w_in)
+    own, to_near, to_far, pay = middle_stage(
+        near, far, x, cot, w_in, wd, z2p, dh2, h1, slope1
+    )
+    dx = own_dx_stage(own, cot, w_in)
     part = first_sum_stage(lax.all_to_all(pay, "sg", 0, 0, tiled=True))
     got = lax.all_to_all(part, "dp", 0, 0, tiled=True)
-    grad_in, grad_out, gg, section_grad = sum_stage(
-        got, shifted(dx, (-1, 0)), shifted(dxl, (-1, -1)), shifted(dxr, (-1, 1))
-    )
+    dx_near, dx_far = pair_dx_stage(to_near, to_far, w_in)
+    dx = sent(dx, 1, lambda plane: plane)
+    dx_far = sent(dx_far, 1, far_of)
+    dx_near = sent(dx_near, 1, near_of)
+    grad_in, grad_out, gg, section_grad = sum_stage(got, dx, dx_near, dx_far)
     return (
         section_grad.reshape(shape),
         grad_in[None],

time: 62.8 us -> 60.9 us (0.970)
  waiting for transfers between devices: 22.3 us -> 19.9 us
  Pallas kernels: 9.73 us -> 10.7 us
    ppermute x5, waiting for transfers between devices: 5.03 us -> 2.6 us  [sent(): return lax.ppermute(value, ('pipe', 'sg'), pairs)]
    pallas_call x5 -> x6, Pallas kernels: 9.73 us -> 10.7 us  [call(): pl.pallas_call(kernel, out_shape=shapes, in_specs=[pl.BlockSpec(memory_sp...]
    all_to_all x1, starting transfers between devices: 8.92 us -> 8.06 us  [per_device(): part = first_sum_stage(lax.all_to_all(pay, 'sg', 0, 0, tiled=True))]
  transfers between devices with their start and end apart: 7 -> 7, of which waited for: 3 -> 4; matrix products, arithmetic and copies ran while one was open for 0% -> 0% of each run, Pallas kernels for 5% -> 6%
where the time goes in v3:
time: 60.9 us; the launch traced here: 60.4 us
  starting transfers between devices  29.1 us (48%)
  waiting for transfers between devices  19.9 us (33%)
  Pallas kernels  10.7 us (18%)
  between operations  0.72 us (1%)
    pallas_call x6, Pallas kernels, call(): pl.pallas_call(kernel, out_shape=shapes, in_specs=[pl.BlockSpec(memory_sp...  10.7 us
    ppermute x5, starting transfers between devices, sent(): return lax.ppermute(value, ('pipe', 'sg'), pairs)  10.7 us
    all_to_all x1, starting transfers between devices, per_device(): got = lax.all_to_all(part, 'dp', 0, 0, tiled=True)  10.4 us
    all_to_all x1, waiting for transfers between devices, per_device(): part = first_sum_stage(lax.all_to_all(pay, 'sg', 0, 0, tiled=True))  9.2 us
    all_to_all x1, starting transfers between devices, per_device(): part = first_sum_stage(lax.all_to_all(pay, 'sg', 0, 0, tiled=True))  8.06 us
    all_to_all x1, waiting for transfers between devices, per_device(): got = lax.all_to_all(part, 'dp', 0, 0, tiled=True)  8.05 us
    ppermute x5, waiting for transfers between devices, sent(): return lax.ppermute(value, ('pipe', 'sg'), pairs)  2.6 us
  transfers between devices with their start and end apart: 7, of which 4 were waited for; matrix products, arithmetic and copies ran while one was open for 0% of the time, Pallas kernels for 6%

profile of v3, /device:TPU:8, one launch (start us, length us, event | category | flops | bytes accessed | tf_op | source)
XLA Modules:
  0.0 60.4 jit_solution(8305741939844462638)
XLA Ops:
  0.6 4.6 %collective-permute-start.1 = (bf16[256,256]{1,0:T(8,128)(2,1)}, bf16[256,256]{1,0:T(8,128)(2,1)S(1)}, u32[]{:S(2)}, u32[]{:S(2)}) collective-permute-start(bf16[256,256]{1,0:T(8,128)(2,1)} %bitcast.12), channel_id=1, source_target_pairs={{1,2},{2,1},{3,4},{4,3},{5,6},{6,5},{7,8},{8,7},{9,10},{10,9},{11,... | collective-permute-start | bytes 393224 | tf_op jit(solution)/shard_map/ppermute | solution.py:322
  5.2 2.2 %collective-permute-start = (bf16[256,256]{1,0:T(8,128)(2,1)}, bf16[256,256]{1,0:T(8,128)(2,1)S(1)}, u32[]{:S(2)}, u32[]{:S(2)}) collective-permute-start(bf16[256,256]{1,0:T(8,128)(2,1)} %bitcast.13), channel_id=1, source_target_pairs={{0,1},{1,0},{2,3},{3,2},{4,5},{5,4},{6,7},{7,6},{8,9},{9,8},{10,11... | collective-permute-start | bytes 393224 | tf_op jit(solution)/shard_map/ppermute | solution.py:322
  7.4 2.2 %shard_map.84 = (f32[256,256]{1,0:T(8,128)S(1)}, bf16[256,256]{1,0:T(8,128)(2,1)S(1)}, bf16[256,256]{1,0:T(8,128)(2,1)S(1)}, bf16[6912,256]{1,0:T(8,128)(2,1)S(1...) custom-call(bf16[256,256]{1,0:T(8,128)(2,1)} %bitcast.14, ...), custom_call_target="tpu_custom_call" | custom-call | flops 369098752 | bytes 5353472 | tf_op jit(solution)/shard_map/pallas_call | solution.py:234
  9.7 0.4 collective-permute-done.1.far
  10.1 2.2 %collective-permute-done.near = bf16[256,256]{1,0:T(8,128)(2,1)S(1)} collective-permute-done((bf16[256,256]{1,0:T(8,128)(2,1)}, bf16[256,256]{1,0:T(8,128)(2,1)S(1)}, u32[]{:S(2)}, u32[]{:S(2)}) %collective-permute-start) | collective-permute-done | bytes 131104 | tf_op jit(solution)/shard_map/ppermute | solution.py:322
  12.3 6.5 %shard_map.85 = (bf16[256,256]{1,0:T(8,128)(2,1)S(1)}, bf16[256,256]{1,0:T(8,128)(2,1)S(1)}, bf16[256,256]{1,0:T(8,128)(2,1)S(1)}, bf16[32,8,768]{2,1,0:T(8,128)(2,1)}) custom-call(bf16[256,256]{1,0:T(8,128)(2,1)S(1)} %collective-permute-done.near, bf16[256,256]{1,0:T(8,128)(2,1)S(1)} %collective-permute-done.1.far, ...), custom_call_target="tpu_custom_call" | custom-call | flops 2684354560 | bytes 5767168 | tf_op jit(solution)/shard_map/pallas_call | solution.py:234
  18.8 8.1 %all-to-all-start = ((bf16[32,8,768]{2,1,0:T(8,128)(2,1)}), bf16[32,8,768]{2,1,0:T(8,128)(2,1)S(1)}, u32[]{:S(2)}, u32[]{:S(2)}) async-start(bf16[32,8,768]{2,1,0:T(8,128)(2,1)} %get-tuple-element.30), calls=%async_computation | async-start | bytes 786432 | tf_op jit(solution)/shard_map/all_to_all | solution.py:343
  26.8 0.3 shard_map.88
  27.1 1.3 %collective-permute-start.3 = (bf16[256,256]{1,0:T(8,128)(2,1)S(1)}, bf16[256,256]{1,0:T(8,128)(2,1)S(1)}, u32[]{:S(2)}, u32[]{:S(2)}) collective-permute-start(bf16[256,256]{1,0:T(8,128)(2,1)S(1)} %get-tuple-element.34), channel_id=1, source_target_pairs={{32,1},{33,0},{34,3},{35,2},{36,5},{37,4},{38,7},{39,6},{40,9},{41... | collective-permute-start | bytes 393224 | tf_op jit(solution)/shard_map/ppermute | solution.py:322
  28.4 0.2 shard_map.87
  28.6 1.3 %collective-permute-start.4 = (bf16[256,256]{1,0:T(8,128)(2,1)S(1)}, bf16[256,256]{1,0:T(8,128)(2,1)S(1)}, u32[]{:S(2)}, u32[]{:S(2)}) collective-permute-start(bf16[256,256]{1,0:T(8,128)(2,1)S(1)} %get-tuple-element.35), channel_id=1, source_target_pairs={{33,2},{34,1},{35,4},{36,3},{37,6},{38,5},{39,8},{40,7},{41,10},{4... | collective-permute-start | bytes 393224 | tf_op jit(solution)/shard_map/ppermute | solution.py:322
  29.9 1.3 %collective-permute-start.2 = (bf16[256,256]{1,0:T(8,128)(2,1)S(1)}, bf16[256,256]{1,0:T(8,128)(2,1)S(1)}, u32[]{:S(2)}, u32[]{:S(2)}) collective-permute-start(bf16[256,256]{1,0:T(8,128)(2,1)S(1)} %shard_map.87), channel_id=1, source_target_pairs={{32,0},{33,1},{34,2},{35,3},{36,4},{37,5},{38,6},{39,7},{40,8},{41... | collective-permute-start | bytes 393224 | tf_op jit(solution)/shard_map/ppermute | solution.py:322
  31.2 9.2 %all-to-all-done.got = bf16[32,8,768]{2,1,0:T(8,128)(2,1)S(1)} async-done(((bf16[32,8,768]{2,1,0:T(8,128)(2,1)}), bf16[32,8,768]{2,1,0:T(8,128)(2,1)S(1)}, u32[]{:S(2)}, u32[]{:S(2)}) %all-to-all-start) | async-done | bytes 393248 | tf_op jit(solution)/shard_map/all_to_all | solution.py:343
  40.4 0.7 %shard_map.86 = f32[4,8,384]{2,1,0:T(8,128)} custom-call(bf16[32,8,768]{2,1,0:T(8,128)(2,1)S(1)} %all-to-all-done.got), custom_call_target="tpu_custom_call" | custom-call | flops 1000 | bytes 442368 | tf_op jit(solution)/shard_map/pallas_call | solution.py:234
  41.1 10.4 %all-to-all-start.1 = ((f32[4,8,384]{2,1,0:T(8,128)}), f32[4,8,384]{2,1,0:T(8,128)S(1)}, u32[]{:S(2)}, u32[]{:S(2)}) async-start(f32[4,8,384]{2,1,0:T(8,128)} %shard_map.86), calls=%async_computation.1 | async-start | bytes 98304 | tf_op jit(solution)/shard_map/all_to_all | solution.py:344
  51.5 0.0 collective-permute-done.3.dxl
  51.5 0.0 collective-permute-done.4.dxr
  51.5 0.0 collective-permute-done.2.dx
  51.5 8.1 %all-to-all-done.1.got = f32[4,8,384]{2,1,0:T(8,128)S(1)} async-done(((f32[4,8,384]{2,1,0:T(8,128)}), f32[4,8,384]{2,1,0:T(8,128)S(1)}, u32[]{:S(2)}, u32[]{:S(2)}) %all-to-all-start.1) | async-done | bytes 49184 | tf_op jit(solution)/shard_map/all_to_all | solution.py:344
  59.6 0.8 %shard_map.89 = (f32[2,256]{1,0:T(2,128)}, f32[2,256]{1,0:T(2,128)}, f32[216,8]{1,0:T(8,128)}, bf16[256,256]{1,0:T(8,128)(2,1)}) custom-call(f32[4,8,384]{2,1,0:T(8,128)S(1)} %all-to-all-done.1.got, bf16[256,256]{1,0:T(8,128)(2,1)S(1)} %collective-permute-done.2.dx, bf16[256,256]{1,0:T(8,128)(2,1)S(1)} %collective-permute-done.3.dxl, ...), custom_call_target="tpu_custom_call" | custom-call | flops 1000 | bytes 584448 | tf_op jit(solution)/shard_map/pallas_call | solution.py:234
Async XLA Ops:
  0.6 9.4 %collective-permute-start.1 = (bf16[256,256]{1,0:T(8,128)(2,1)}, bf16[256,256]{1,0:T(8,128)(2,1)S(1)}, u32[]{:S(2)}, u32[]{:S(2)}) collective-permute-start(bf16[256,256]{1,0:T(8,128)(2,1)} %bitcast.12), channel_id=1, source_target_pairs={{1,2},{2,1},{3,4},{4,3},{5,6},{6,5},{7,8},{8,7},{9,10},{10,9},{11,... | collective-permute-start | bytes 393224 | tf_op jit(solution)/shard_map/ppermute | solution.py:322
  5.2 7.1 %collective-permute-start = (bf16[256,256]{1,0:T(8,128)(2,1)}, bf16[256,256]{1,0:T(8,128)(2,1)S(1)}, u32[]{:S(2)}, u32[]{:S(2)}) collective-permute-start(bf16[256,256]{1,0:T(8,128)(2,1)} %bitcast.13), channel_id=1, source_target_pairs={{0,1},{1,0},{2,3},{3,2},{4,5},{5,4},{6,7},{7,6},{8,9},{9,8},{10,11... | collective-permute-start | bytes 393224 | tf_op jit(solution)/shard_map/ppermute | solution.py:322
  18.8 21.7 %all-to-all-start = ((bf16[32,8,768]{2,1,0:T(8,128)(2,1)}), bf16[32,8,768]{2,1,0:T(8,128)(2,1)S(1)}, u32[]{:S(2)}, u32[]{:S(2)}) async-start(bf16[32,8,768]{2,1,0:T(8,128)(2,1)} %get-tuple-element.30), calls=%async_computation | async-start | bytes 786432 | tf_op jit(solution)/shard_map/all_to_all | solution.py:343
  27.1 24.4 %collective-permute-start.3 = (bf16[256,256]{1,0:T(8,128)(2,1)S(1)}, bf16[256,256]{1,0:T(8,128)(2,1)S(1)}, u32[]{:S(2)}, u32[]{:S(2)}) collective-permute-start(bf16[256,256]{1,0:T(8,128)(2,1)S(1)} %get-tuple-element.34), channel_id=1, source_target_pairs={{32,1},{33,0},{34,3},{35,2},{36,5},{37,4},{38,7},{39,6},{40,9},{41... | collective-permute-start | bytes 393224 | tf_op jit(solution)/shard_map/ppermute | solution.py:322
  28.6 22.9 %collective-permute-start.4 = (bf16[256,256]{1,0:T(8,128)(2,1)S(1)}, bf16[256,256]{1,0:T(8,128)(2,1)S(1)}, u32[]{:S(2)}, u32[]{:S(2)}) collective-permute-start(bf16[256,256]{1,0:T(8,128)(2,1)S(1)} %get-tuple-element.35), channel_id=1, source_target_pairs={{33,2},{34,1},{35,4},{36,3},{37,6},{38,5},{39,8},{40,7},{41,10},{4... | collective-permute-start | bytes 393224 | tf_op jit(solution)/shard_map/ppermute | solution.py:322
  29.9 21.6 %collective-permute-start.2 = (bf16[256,256]{1,0:T(8,128)(2,1)S(1)}, bf16[256,256]{1,0:T(8,128)(2,1)S(1)}, u32[]{:S(2)}, u32[]{:S(2)}) collective-permute-start(bf16[256,256]{1,0:T(8,128)(2,1)S(1)} %shard_map.87), channel_id=1, source_target_pairs={{32,0},{33,1},{34,2},{35,3},{36,4},{37,5},{38,6},{39,7},{40,8},{41... | collective-permute-start | bytes 393224 | tf_op jit(solution)/shard_map/ppermute | solution.py:322
  41.1 18.4 %all-to-all-start.1 = ((f32[4,8,384]{2,1,0:T(8,128)}), f32[4,8,384]{2,1,0:T(8,128)S(1)}, u32[]{:S(2)}, u32[]{:S(2)}) async-start(f32[4,8,384]{2,1,0:T(8,128)} %shard_map.86), calls=%async_computation.1 | async-start | bytes 98304 | tf_op jit(solution)/shard_map/all_to_all | solution.py:344

commit v4 on v3

--- a/solution.py
+++ b/solution.py
@@ -51,11 +51,15 @@
     buf[SIDE : SIDE + CELLS, 2 * C :] = right.astype(BF16)
 
 
+def tap(depth, row, col=0):
+    start = ((depth * 3 + row) * 3 + col) * C
+    return start if isinstance(start, int) else pl.multiple_of(start, C)
+
+
 def conv_plane(buf, wd, depth):
     total = None
     for row in range(3):
-        start = (depth * 3 + row) * 3 * C
-        term = dot(buf[row * SIDE : row * SIDE + CELLS, :], wd[start : start + 3 * C, :])
+        term = dot(buf[row * SIDE : row * SIDE + CELLS, :], wd[pl.ds(tap(depth, row), 3 * C), :])
         total = term if total is None else total + term
     return total
 
@@ -64,13 +68,32 @@
     total = None
     for row in range(3):
         for col in range(3):
-            start = ((depth * 3 + row) * 3 + col) * C
             rows = (2 - row) * SIDE
             term = dot_nt(
-                buf[rows : rows + CELLS, col * C : (col + 1) * C], wd[start : start + C, :]
+                buf[rows : rows + CELLS, col * C : (col + 1) * C],
+                wd[pl.ds(tap(depth, row, col), C), :],
             )
             total = term if total is None else total + term
     return total
+
+
+def neighbour_depths():
+    odd = lax.axis_index("sg") % 2
+    return 2 - 2 * odd, 2 * odd
+
+
+def activate(x, w_in):
+    z1 = dot(x[...], w_in[...])
+    sig = sigmoid(z1)
+    return (z1 * sig).astype(BF16), sig * (1.0 + z1 * (1.0 - sig))
+
+
+def far_kernel(far, w_in, wd, z2p, h1, slope, total, buf):
+    act, grad = activate(far, w_in)
+    slope[...] = grad
+    h1[...] = act
+    fill(buf, act.astype(F32), 1)
+    total[...] = z2p[...] + conv_plane(buf, wd, neighbour_depths()[1])
 
 
 def spread(wg, wd, which):
@@ -101,10 +124,8 @@
     spread(wg, wd, range(TAPS))
     for copy in copies[1:]:
         copy.wait()
-    z1 = dot(x[...], w_in[...])
-    sig = sigmoid(z1)
-    slope1[...] = sig * (1.0 + z1 * (1.0 - sig))
-    act = (z1 * sig).astype(BF16)
+    act, grad = activate(x, w_in)
+    slope1[...] = grad
     h1[...] = act
     dh2[...] = dot_nt(cot[...], w_out[...]).astype(BF16)
     fill(buf, act.astype(F32), 1)
@@ -112,32 +133,16 @@
 
 
 def middle_kernel(
-    near, far, x, cot, w_in, wd, z2p, dh2, h1, slope1,
+    near, far, x, cot, w_in, wd, z2f, dh2, h1, slope1, h1f, slopef,
     own, to_near, to_far, pay,
-    bufl, bufr, buf, ht, slopes, taps, grads, pack, xl, xr, left, right,
+    bufn, buf, ht, slopen, taps, grads, pack,
 ):
     half = C // 2
-    even = lax.axis_index("sg") % 2 == 0
-
-    def swap(pair, out):
-        @pl.when(even)
-        def _():
-            out[0][...] = pair[1][...]
-            out[1][...] = pair[0][...]
-
-        @pl.when(jnp.logical_not(even))
-        def _():
-            out[0][...] = pair[0][...]
-            out[1][...] = pair[1][...]
-
-    swap((near, far), (xl, xr))
-    total = z2p[...]
-    for x_next, b, depth in ((xl, bufl, 0), (xr, bufr, 2)):
-        z1 = dot(x_next[...], w_in[...])
-        sig = sigmoid(z1)
-        slopes[depth // 2] = sig * (1.0 + z1 * (1.0 - sig))
-        fill(b, (z1 * sig).astype(BF16).astype(F32), 1)
-        total = total + conv_plane(b, wd, depth)
+    depth_near, depth_far = neighbour_depths()
+    act, grad = activate(near, w_in)
+    slopen[...] = grad
+    fill(bufn, act.astype(F32), 1)
+    total = z2f[...] + conv_plane(bufn, wd, depth_near)
     sig = sigmoid(total)
     h2 = (total * sig).astype(BF16)
     slope = sig * (1.0 + total * (1.0 - sig))
@@ -149,18 +154,20 @@
     share = (conv_plane_back(buf, wd, 1) * slope1[...]).astype(BF16)
     own[...] = share
     outer = dot(x[...].T, share)
-    for x_next, out, depth in ((xl, left, 0), (xr, right, 2)):
-        share = (conv_plane_back(buf, wd, depth) * slopes[depth // 2]).astype(BF16)
+    for x_next, out, slope, depth in (
+        (far, to_far, slopef, depth_far),
+        (near, to_near, slopen, depth_near),
+    ):
+        share = (conv_plane_back(buf, wd, depth) * slope[...]).astype(BF16)
         outer = outer + dot(x_next[...].T, share)
         out[...] = share
-    swap((left, right), (to_near, to_far))
     for side in range(2):
         grads[side] = outer[:, side * half : (side + 1) * half]
-    for depth, plane in enumerate((bufl, None, bufr)):
-        value = h1[...] if plane is None else plane[SIDE : SIDE + CELLS, C : 2 * C]
+    for which, plane in enumerate((h1f, h1, None)):
+        value = bufn[SIDE : SIDE + CELLS, C : 2 * C] if plane is None else plane[...]
         turned = value.T
         for side in range(2):
-            ht[side, depth * half : (depth + 1) * half, :] = turned[
+            ht[side, which * half : (which + 1) * half, :] = turned[
                 side * half : (side + 1) * half, :
             ]
     groups = half // GW
@@ -175,10 +182,10 @@
             for side in range(2):
                 lanes = col * C + side * half
                 full = dot(ht[side], buf[rows : rows + CELLS, lanes : lanes + half])
-                for depth in range(3):
-                    block = jnp.where(same, full[depth * half : (depth + 1) * half, :], 0.0)
-                    k = (depth * 3 + row) * 3 + col
-                    taps[k * GW : (k + 1) * GW, side * half : (side + 1) * half] = jnp.sum(
+                for which, depth in enumerate((depth_far, 1, depth_near)):
+                    block = jnp.where(same, full[which * half : (which + 1) * half, :], 0.0)
+                    first = ((depth * 3 + row) * 3 + col) * GW
+                    taps[pl.ds(first, GW), side * half : (side + 1) * half] = jnp.sum(
                         block.reshape(groups, GW, half), axis=0
                     )
     for which in range(2):
@@ -263,20 +270,26 @@
     )
 
 
+def far_stage(*args):
+    return call(
+        far_kernel, [(PLANE, BF16), (PLANE, F32), (PLANE, F32)], [BUF], 10 * TILE, *args
+    )
+
+
 def middle_stage(*args):
     return call(
         middle_kernel,
         [(PLANE, BF16)] * 3 + [(PAY, BF16)],
         [
-            BUF, BUF, BUF,
+            BUF,
+            BUF,
             ((2, 3 * C // 2, CELLS), BF16),
-            ((2, CELLS, C), F32),
-            ((C, C), F32),
+            (PLANE, F32),
+            (PLANE, F32),
             ((4, C, C // 2), F32),
             ((NDEV * 8, C // 2), F32),
-        ]
-        + [(PLANE, BF16)] * 4,
-        80 * TILE,
+        ],
+        70 * TILE,
         *args,
     )
 
@@ -336,8 +349,9 @@
         for value in (x, cot, w_in, w_out, wg)
     ]
     slope1, h1, dh2, wd, z2p, x, cot, w_in = own_stage(*kept)
+    h1f, slopef, z2f = far_stage(far, w_in, wd, z2p)
     own, to_near, to_far, pay = middle_stage(
-        near, far, x, cot, w_in, wd, z2p, dh2, h1, slope1
+        near, far, x, cot, w_in, wd, z2f, dh2, h1, slope1, h1f, slopef
     )
     dx = own_dx_stage(own, cot, w_in)
     part = first_sum_stage(lax.all_to_all(pay, "sg", 0, 0, tiled=True))

time: 60.9 us -> 59.8 us (0.982)
  the two profiles are of different devices: /device:TPU:8 before, /device:TPU:64 now
where the time goes in v4:
time: 59.8 us; the launch traced here: 59.3 us
  starting transfers between devices  31.5 us (53%)
  waiting for transfers between devices  17.7 us (30%)
  Pallas kernels  9.42 us (16%)
  between operations  0.73 us (1%)
    ppermute x5, starting transfers between devices, sent(): return lax.ppermute(value, ('pipe', 'sg'), pairs)  12.4 us
    all_to_all x1, starting transfers between devices, per_device(): part = first_sum_stage(lax.all_to_all(pay, 'sg', 0, 0, tiled=True))  9.63 us
    pallas_call x7, Pallas kernels, call(): pl.pallas_call(kernel, out_shape=shapes, in_specs=[pl.BlockSpec(memory_sp...  9.42 us
    all_to_all x1, starting transfers between devices, per_device(): got = lax.all_to_all(part, 'dp', 0, 0, tiled=True)  9.39 us
    all_to_all x1, waiting for transfers between devices, per_device(): part = first_sum_stage(lax.all_to_all(pay, 'sg', 0, 0, tiled=True))  9.15 us
    all_to_all x1, waiting for transfers between devices, per_device(): got = lax.all_to_all(part, 'dp', 0, 0, tiled=True)  8.05 us
  transfers between devices with their start and end apart: 7, of which 3 were waited for; matrix products, arithmetic and copies ran while one was open for 0% of the time, Pallas kernels for 7%

profile of v4, /device:TPU:64, one launch (start us, length us, event | category | flops | bytes accessed | tf_op | source)
XLA Modules:
  0.0 59.3 jit_solution(17973411418855896460)
XLA Ops:
  0.6 0.7 %collective-permute-start.1 = (bf16[256,256]{1,0:T(8,128)(2,1)}, bf16[256,256]{1,0:T(8,128)(2,1)S(1)}, u32[]{:S(2)}, u32[]{:S(2)}) collective-permute-start(bf16[256,256]{1,0:T(8,128)(2,1)} %bitcast.12), channel_id=1, source_target_pairs={{1,2},{2,1},{3,4},{4,3},{5,6},{6,5},{7,8},{8,7},{9,10},{10,9},{11,... | collective-permute-start | bytes 393224 | tf_op jit(solution)/shard_map/ppermute | solution.py:335
  1.3 6.1 %collective-permute-start = (bf16[256,256]{1,0:T(8,128)(2,1)}, bf16[256,256]{1,0:T(8,128)(2,1)S(1)}, u32[]{:S(2)}, u32[]{:S(2)}) collective-permute-start(bf16[256,256]{1,0:T(8,128)(2,1)} %bitcast.13), channel_id=1, source_target_pairs={{0,1},{1,0},{2,3},{3,2},{4,5},{5,4},{6,7},{7,6},{8,9},{9,8},{10,11... | collective-permute-start | bytes 393224 | tf_op jit(solution)/shard_map/ppermute | solution.py:335
  7.4 2.2 %shard_map.84 = (f32[256,256]{1,0:T(8,128)S(1)}, bf16[256,256]{1,0:T(8,128)(2,1)S(1)}, bf16[256,256]{1,0:T(8,128)(2,1)S(1)}, bf16[6912,256]{1,0:T(8,128)(2,1)S(1...) custom-call(bf16[256,256]{1,0:T(8,128)(2,1)} %bitcast.14, ...), custom_call_target="tpu_custom_call" | custom-call | flops 369098752 | bytes 5353472 | tf_op jit(solution)/shard_map/pallas_call | solution.py:241
  9.7 0.0 collective-permute-done.1.far
  9.7 0.7 %shard_map.85 = (bf16[256,256]{1,0:T(8,128)(2,1)S(1)}, f32[256,256]{1,0:T(8,128)S(1)}, f32[256,256]{1,0:T(8,128)S(1)}) custom-call(bf16[256,256]{1,0:T(8,128)(2,1)S(1)} %collective-permute-done.1.far, bf16[256,256]{1,0:T(8,128)(2,1)S(1)} %get-tuple-element.27.w_in, bf16[6912,256]{1,0:T(8,128)(2,1)S(1)} %get-tuple-element.28.wd, ...), custom_call_target="tpu_custom_call" | custom-call | flops 335544320 | bytes 4718592 | tf_op jit(solution)/shard_map/pallas_call | solution.py:241
  10.4 0.5 collective-permute-done.near
  10.9 4.5 %shard_map.86 = (bf16[256,256]{1,0:T(8,128)(2,1)S(1)}, bf16[256,256]{1,0:T(8,128)(2,1)S(1)}, bf16[256,256]{1,0:T(8,128)(2,1)S(1)}, bf16[32,8,768]{2,1,0:T(8,128)(2,1)}) custom-call(bf16[256,256]{1,0:T(8,128)(2,1)S(1)} %collective-permute-done.near, bf16[256,256]{1,0:T(8,128)(2,1)S(1)} %collective-permute-done.1.far, ...), custom_call_target="tpu_custom_call" | custom-call | flops 2348810240 | bytes 6160384 | tf_op jit(solution)/shard_map/pallas_call | solution.py:241
  15.4 9.6 %all-to-all-start = ((bf16[32,8,768]{2,1,0:T(8,128)(2,1)}), bf16[32,8,768]{2,1,0:T(8,128)(2,1)S(1)}, u32[]{:S(2)}, u32[]{:S(2)}) async-start(bf16[32,8,768]{2,1,0:T(8,128)(2,1)} %get-tuple-element.36), calls=%async_computation | async-start | bytes 786432 | tf_op jit(solution)/shard_map/all_to_all | solution.py:357
  25.0 0.3 shard_map.89
  25.3 1.9 %collective-permute-start.3 = (bf16[256,256]{1,0:T(8,128)(2,1)S(1)}, bf16[256,256]{1,0:T(8,128)(2,1)S(1)}, u32[]{:S(2)}, u32[]{:S(2)}) collective-permute-start(bf16[256,256]{1,0:T(8,128)(2,1)S(1)} %get-tuple-element.40), channel_id=1, source_target_pairs={{32,1},{33,0},{34,3},{35,2},{36,5},{37,4},{38,7},{39,6},{40,9},{41... | collective-permute-start | bytes 393224 | tf_op jit(solution)/shard_map/ppermute | solution.py:335
  27.2 0.2 shard_map.88
  27.4 0.7 %collective-permute-start.4 = (bf16[256,256]{1,0:T(8,128)(2,1)S(1)}, bf16[256,256]{1,0:T(8,128)(2,1)S(1)}, u32[]{:S(2)}, u32[]{:S(2)}) collective-permute-start(bf16[256,256]{1,0:T(8,128)(2,1)S(1)} %get-tuple-element.41), channel_id=1, source_target_pairs={{33,2},{34,1},{35,4},{36,3},{37,6},{38,5},{39,8},{40,7},{41,10},{4... | collective-permute-start | bytes 393224 | tf_op jit(solution)/shard_map/ppermute | solution.py:335
  28.1 3.1 %collective-permute-start.2 = (bf16[256,256]{1,0:T(8,128)(2,1)S(1)}, bf16[256,256]{1,0:T(8,128)(2,1)S(1)}, u32[]{:S(2)}, u32[]{:S(2)}) collective-permute-start(bf16[256,256]{1,0:T(8,128)(2,1)S(1)} %shard_map.88), channel_id=1, source_target_pairs={{32,0},{33,1},{34,2},{35,3},{36,4},{37,5},{38,6},{39,7},{40,8},{41... | collective-permute-start | bytes 393224 | tf_op jit(solution)/shard_map/ppermute | solution.py:335
  31.2 9.1 %all-to-all-done.got = bf16[32,8,768]{2,1,0:T(8,128)(2,1)S(1)} async-done(((bf16[32,8,768]{2,1,0:T(8,128)(2,1)}), bf16[32,8,768]{2,1,0:T(8,128)(2,1)S(1)}, u32[]{:S(2)}, u32[]{:S(2)}) %all-to-all-start) | async-done | bytes 393248 | tf_op jit(solution)/shard_map/all_to_all | solution.py:357
  40.3 0.7 %shard_map.87 = f32[4,8,384]{2,1,0:T(8,128)} custom-call(bf16[32,8,768]{2,1,0:T(8,128)(2,1)S(1)} %all-to-all-done.got), custom_call_target="tpu_custom_call" | custom-call | flops 1000 | bytes 442368 | tf_op jit(solution)/shard_map/pallas_call | solution.py:241
  41.0 9.4 %all-to-all-start.1 = ((f32[4,8,384]{2,1,0:T(8,128)}), f32[4,8,384]{2,1,0:T(8,128)S(1)}, u32[]{:S(2)}, u32[]{:S(2)}) async-start(f32[4,8,384]{2,1,0:T(8,128)} %shard_map.87), calls=%async_computation.1 | async-start | bytes 98304 | tf_op jit(solution)/shard_map/all_to_all | solution.py:358
  50.4 0.0 collective-permute-done.3.dxl
  50.4 0.0 collective-permute-done.4.dxr
  50.4 0.0 collective-permute-done.2.dx
  50.4 8.1 %all-to-all-done.1.got = f32[4,8,384]{2,1,0:T(8,128)S(1)} async-done(((f32[4,8,384]{2,1,0:T(8,128)}), f32[4,8,384]{2,1,0:T(8,128)S(1)}, u32[]{:S(2)}, u32[]{:S(2)}) %all-to-all-start.1) | async-done | bytes 49184 | tf_op jit(solution)/shard_map/all_to_all | solution.py:358
  58.5 0.8 %shard_map.90 = (f32[2,256]{1,0:T(2,128)}, f32[2,256]{1,0:T(2,128)}, f32[216,8]{1,0:T(8,128)}, bf16[256,256]{1,0:T(8,128)(2,1)}) custom-call(f32[4,8,384]{2,1,0:T(8,128)S(1)} %all-to-all-done.1.got, bf16[256,256]{1,0:T(8,128)(2,1)S(1)} %collective-permute-done.2.dx, bf16[256,256]{1,0:T(8,128)(2,1)S(1)} %collective-permute-done.3.dxl, ...), custom_call_target="tpu_custom_call" | custom-call | flops 1000 | bytes 584448 | tf_op jit(solution)/shard_map/pallas_call | solution.py:241
Async XLA Ops:
  0.6 9.0 %collective-permute-start.1 = (bf16[256,256]{1,0:T(8,128)(2,1)}, bf16[256,256]{1,0:T(8,128)(2,1)S(1)}, u32[]{:S(2)}, u32[]{:S(2)}) collective-permute-start(bf16[256,256]{1,0:T(8,128)(2,1)} %bitcast.12), channel_id=1, source_target_pairs={{1,2},{2,1},{3,4},{4,3},{5,6},{6,5},{7,8},{8,7},{9,10},{10,9},{11,... | collective-permute-start | bytes 393224 | tf_op jit(solution)/shard_map/ppermute | solution.py:335
  1.3 9.5 %collective-permute-start = (bf16[256,256]{1,0:T(8,128)(2,1)}, bf16[256,256]{1,0:T(8,128)(2,1)S(1)}, u32[]{:S(2)}, u32[]{:S(2)}) collective-permute-start(bf16[256,256]{1,0:T(8,128)(2,1)} %bitcast.13), channel_id=1, source_target_pairs={{0,1},{1,0},{2,3},{3,2},{4,5},{5,4},{6,7},{7,6},{8,9},{9,8},{10,11... | collective-permute-start | bytes 393224 | tf_op jit(solution)/shard_map/ppermute | solution.py:335
  15.4 25.0 %all-to-all-start = ((bf16[32,8,768]{2,1,0:T(8,128)(2,1)}), bf16[32,8,768]{2,1,0:T(8,128)(2,1)S(1)}, u32[]{:S(2)}, u32[]{:S(2)}) async-start(bf16[32,8,768]{2,1,0:T(8,128)(2,1)} %get-tuple-element.36), calls=%async_computation | async-start | bytes 786432 | tf_op jit(solution)/shard_map/all_to_all | solution.py:357
  25.3 25.1 %collective-permute-start.3 = (bf16[256,256]{1,0:T(8,128)(2,1)S(1)}, bf16[256,256]{1,0:T(8,128)(2,1)S(1)}, u32[]{:S(2)}, u32[]{:S(2)}) collective-permute-start(bf16[256,256]{1,0:T(8,128)(2,1)S(1)} %get-tuple-element.40), channel_id=1, source_target_pairs={{32,1},{33,0},{34,3},{35,2},{36,5},{37,4},{38,7},{39,6},{40,9},{41... | collective-permute-start | bytes 393224 | tf_op jit(solution)/shard_map/ppermute | solution.py:335
  27.4 23.0 %collective-permute-start.4 = (bf16[256,256]{1,0:T(8,128)(2,1)S(1)}, bf16[256,256]{1,0:T(8,128)(2,1)S(1)}, u32[]{:S(2)}, u32[]{:S(2)}) collective-permute-start(bf16[256,256]{1,0:T(8,128)(2,1)S(1)} %get-tuple-element.41), channel_id=1, source_target_pairs={{33,2},{34,1},{35,4},{36,3},{37,6},{38,5},{39,8},{40,7},{41,10},{4... | collective-permute-start | bytes 393224 | tf_op jit(solution)/shard_map/ppermute | solution.py:335
  28.1 22.3 %collective-permute-start.2 = (bf16[256,256]{1,0:T(8,128)(2,1)S(1)}, bf16[256,256]{1,0:T(8,128)(2,1)S(1)}, u32[]{:S(2)}, u32[]{:S(2)}) collective-permute-start(bf16[256,256]{1,0:T(8,128)(2,1)S(1)} %shard_map.88), channel_id=1, source_target_pairs={{32,0},{33,1},{34,2},{35,3},{36,4},{37,5},{38,6},{39,7},{40,8},{41... | collective-permute-start | bytes 393224 | tf_op jit(solution)/shard_map/ppermute | solution.py:335
  41.0 17.5 %all-to-all-start.1 = ((f32[4,8,384]{2,1,0:T(8,128)}), f32[4,8,384]{2,1,0:T(8,128)S(1)}, u32[]{:S(2)}, u32[]{:S(2)}) async-start(f32[4,8,384]{2,1,0:T(8,128)} %shard_map.87), calls=%async_computation.1 | async-start | bytes 98304 | tf_op jit(solution)/shard_map/all_to_all | solution.py:358

commit v5 on v4

--- a/solution.py
+++ b/solution.py
@@ -51,6 +51,27 @@
     buf[SIDE : SIDE + CELLS, 2 * C :] = right.astype(BF16)
 
 
+def conv_shifted(rows, wd, depth):
+    sums = []
+    for col in range(3):
+        total = None
+        for row in range(3):
+            term = dot(rows[row * SIDE : row * SIDE + CELLS, :], wd[pl.ds(tap(depth, row, col), C), :])
+            total = term if total is None else total + term
+        sums.append(total)
+    at = column()
+    behind = jnp.where(at > 0, pltpu.roll(sums[0], 1, 0), 0.0)
+    ahead = jnp.where(at < SIDE - 1, pltpu.roll(sums[2], CELLS - 1, 0), 0.0)
+    return sums[1] + (behind + ahead)
+
+
+def keep_rows(rows, plane):
+    zeros = jnp.zeros((SIDE, C), BF16)
+    rows[0:SIDE, :] = zeros
+    rows[SIDE : SIDE + CELLS, :] = plane
+    rows[SIDE + CELLS :, :] = zeros
+
+
 def tap(depth, row, col=0):
     start = ((depth * 3 + row) * 3 + col) * C
     return start if isinstance(start, int) else pl.multiple_of(start, C)
@@ -88,12 +109,13 @@
     return (z1 * sig).astype(BF16), sig * (1.0 + z1 * (1.0 - sig))
 
 
-def far_kernel(far, w_in, wd, z2p, h1, slope, total, buf):
+def far_kernel(far, w_in, wd, z2p, h1t, slope, total, far_t, buf):
     act, grad = activate(far, w_in)
     slope[...] = grad
-    h1[...] = act
-    fill(buf, act.astype(F32), 1)
-    total[...] = z2p[...] + conv_plane(buf, wd, neighbour_depths()[1])
+    h1t[...] = act.T
+    far_t[...] = far[...].T
+    keep_rows(buf, act)
+    total[...] = z2p[...] + conv_shifted(buf, wd, neighbour_depths()[1])
 
 
 def spread(wg, wd, which):
@@ -109,8 +131,8 @@
 
 def own_kernel(
     x_hbm, cot_hbm, w_in_hbm, w_out_hbm, wg_hbm,
-    slope1, h1, dh2, wd, z2p, x, cot, w_in,
-    buf, w_out, wg, sems,
+    slope1, h1t, dh2, wd, z2p, xt, cot, w_in,
+    x, buf, w_out, wg, sems,
 ):
     copies = [
         pltpu.make_async_copy(source, target, sems.at[i])
@@ -126,14 +148,15 @@
         copy.wait()
     act, grad = activate(x, w_in)
     slope1[...] = grad
-    h1[...] = act
+    h1t[...] = act.T
+    xt[...] = x[...].T
     dh2[...] = dot_nt(cot[...], w_out[...]).astype(BF16)
-    fill(buf, act.astype(F32), 1)
-    z2p[...] = conv_plane(buf, wd, 1)
+    keep_rows(buf, act)
+    z2p[...] = conv_shifted(buf, wd, 1)
 
 
 def middle_kernel(
-    near, far, x, cot, w_in, wd, z2f, dh2, h1, slope1, h1f, slopef,
+    near, far_t, xt, cot, w_in, wd, z2f, dh2, h1t, slope1, h1ft, slopef,
     own, to_near, to_far, pay,
     bufn, buf, ht, slopen, taps, grads, pack,
 ):
@@ -141,8 +164,8 @@
     depth_near, depth_far = neighbour_depths()
     act, grad = activate(near, w_in)
     slopen[...] = grad
-    fill(bufn, act.astype(F32), 1)
-    total = z2f[...] + conv_plane(bufn, wd, depth_near)
+    keep_rows(bufn, act)
+    total = z2f[...] + conv_shifted(bufn, wd, depth_near)
     sig = sigmoid(total)
     h2 = (total * sig).astype(BF16)
     slope = sig * (1.0 + total * (1.0 - sig))
@@ -153,19 +176,17 @@
         grads[2 + side] = outer[:, side * half : (side + 1) * half]
     share = (conv_plane_back(buf, wd, 1) * slope1[...]).astype(BF16)
     own[...] = share
-    outer = dot(x[...].T, share)
-    for x_next, out, slope, depth in (
-        (far, to_far, slopef, depth_far),
-        (near, to_near, slopen, depth_near),
+    outer = dot(xt[...], share)
+    for turned, out, slope, depth in (
+        (far_t[...], to_far, slopef, depth_far),
+        (near[...].T, to_near, slopen, depth_near),
     ):
         share = (conv_plane_back(buf, wd, depth) * slope[...]).astype(BF16)
-        outer = outer + dot(x_next[...].T, share)
+        outer = outer + dot(turned, share)
         out[...] = share
     for side in range(2):
         grads[side] = outer[:, side * half : (side + 1) * half]
-    for which, plane in enumerate((h1f, h1, None)):
-        value = bufn[SIDE : SIDE + CELLS, C : 2 * C] if plane is None else plane[...]
-        turned = value.T
+    for which, turned in enumerate((h1ft[...], h1t[...], act.T)):
         for side in range(2):
             ht[side, which * half : (which + 1) * half, :] = turned[
                 side * half : (side + 1) * half, :
@@ -177,13 +198,23 @@
     )
     taps[TAPS * GW :, :] = jnp.zeros((C - TAPS * GW, C), F32)
     for row in range(3):
-        for col in range(3):
-            rows = (2 - row) * SIDE
-            for side in range(2):
-                lanes = col * C + side * half
-                full = dot(ht[side], buf[rows : rows + CELLS, lanes : lanes + half])
+        rows = (2 - row) * SIDE
+        for side in range(2):
+            wide = jnp.concatenate(
+                [
+                    buf[rows : rows + CELLS, col * C + side * half : col * C + (side + 1) * half]
+                    for col in range(3)
+                ],
+                axis=1,
+            )
+            full = dot(ht[side], wide)
+            for col in range(3):
                 for which, depth in enumerate((depth_far, 1, depth_near)):
-                    block = jnp.where(same, full[which * half : (which + 1) * half, :], 0.0)
+                    block = jnp.where(
+                        same,
+                        full[which * half : (which + 1) * half, col * half : (col + 1) * half],
+                        0.0,
+                    )
                     first = ((depth * 3 + row) * 3 + col) * GW
                     taps[pl.ds(first, GW), side * half : (side + 1) * half] = jnp.sum(
                         block.reshape(groups, GW, half), axis=0
@@ -263,7 +294,7 @@
         own_kernel,
         [(PLANE, F32), (PLANE, BF16), (PLANE, BF16), ((TAPS * C, C), BF16), (PLANE, F32)]
         + [(PLANE, BF16)] * 3,
-        [BUF, (PLANE, BF16), ((TAPS * GW, C), BF16), pltpu.SemaphoreType.DMA((5,))],
+        [(PLANE, BF16), ((PAD_ROWS, C), BF16), (PLANE, BF16), ((TAPS * GW, C), BF16), pltpu.SemaphoreType.DMA((5,))],
         11 * TILE,
         x, cot, w_in, w_out, wg,
         space=pltpu.HBM,
@@ -272,7 +303,7 @@
 
 def far_stage(*args):
     return call(
-        far_kernel, [(PLANE, BF16), (PLANE, F32), (PLANE, F32)], [BUF], 10 * TILE, *args
+        far_kernel, [(PLANE, BF16), (PLANE, F32), (PLANE, F32), (PLANE, BF16)], [((PAD_ROWS, C), BF16)], 10 * TILE, *args
     )
 
 
@@ -281,7 +312,7 @@
         middle_kernel,
         [(PLANE, BF16)] * 3 + [(PAY, BF16)],
         [
-            BUF,
+            ((PAD_ROWS, C), BF16),
             BUF,
             ((2, 3 * C // 2, CELLS), BF16),
             (PLANE, F32),
@@ -348,10 +379,10 @@
         pltpu.with_memory_space_constraint(value, pltpu.HBM)
         for value in (x, cot, w_in, w_out, wg)
     ]
-    slope1, h1, dh2, wd, z2p, x, cot, w_in = own_stage(*kept)
-    h1f, slopef, z2f = far_stage(far, w_in, wd, z2p)
+    slope1, h1t, dh2, wd, z2p, xt, cot, w_in = own_stage(*kept)
+    h1ft, slopef, z2f, far_t = far_stage(far, w_in, wd, z2p)
     own, to_near, to_far, pay = middle_stage(
-        near, far, x, cot, w_in, wd, z2f, dh2, h1, slope1, h1f, slopef
+        near, far_t, xt, cot, w_in, wd, z2f, dh2, h1t, slope1, h1ft, slopef
     )
     dx = own_dx_stage(own, cot, w_in)
     part = first_sum_stage(lax.all_to_all(pay, "sg", 0, 0, tiled=True))

time: 59.8 us -> 59.3 us (level)
  the two profiles are of different devices: /device:TPU:64 before, /device:TPU:8 now
where the time goes in v5:
time: 59.3 us; the launch traced here: 58.6 us
  starting transfers between devices  29.4 us (50%)
  waiting for transfers between devices  19.7 us (33%)
  Pallas kernels  8.84 us (15%)
  between operations  0.72 us (1%)
    ppermute x5, starting transfers between devices, sent(): return lax.ppermute(value, ('pipe', 'sg'), pairs)  10.7 us
    all_to_all x1, starting transfers between devices, per_device(): got = lax.all_to_all(part, 'dp', 0, 0, tiled=True)  10.3 us
    all_to_all x1, waiting for transfers between devices, per_device(): part = first_sum_stage(lax.all_to_all(pay, 'sg', 0, 0, tiled=True))  9.51 us
    pallas_call x7, Pallas kernels, call(): pl.pallas_call(kernel, out_shape=shapes, in_specs=[pl.BlockSpec(memory_sp...  8.84 us
    all_to_all x1, starting transfers between devices, per_device(): part = first_sum_stage(lax.all_to_all(pay, 'sg', 0, 0, tiled=True))  8.42 us
    all_to_all x1, waiting for transfers between devices, per_device(): got = lax.all_to_all(part, 'dp', 0, 0, tiled=True)  8.11 us
    ppermute x5, waiting for transfers between devices, sent(): return lax.ppermute(value, ('pipe', 'sg'), pairs)  2.05 us
  transfers between devices with their start and end apart: 7, of which 4 were waited for; matrix products, arithmetic and copies ran while one was open for 0% of the time, Pallas kernels for 7%

profile of v5, /device:TPU:8, one launch (start us, length us, event | category | flops | bytes accessed | tf_op | source)
XLA Modules:
  0.0 58.6 jit_solution(473803145120438506)
XLA Ops:
  0.6 4.6 %collective-permute-start.1 = (bf16[256,256]{1,0:T(8,128)(2,1)}, bf16[256,256]{1,0:T(8,128)(2,1)S(1)}, u32[]{:S(2)}, u32[]{:S(2)}) collective-permute-start(bf16[256,256]{1,0:T(8,128)(2,1)} %bitcast.12), channel_id=1, source_target_pairs={{1,2},{2,1},{3,4},{4,3},{5,6},{6,5},{7,8},{8,7},{9,10},{10,9},{11,... | collective-permute-start | bytes 393224 | tf_op jit(solution)/shard_map/ppermute | solution.py:366
  5.2 2.2 %collective-permute-start = (bf16[256,256]{1,0:T(8,128)(2,1)}, bf16[256,256]{1,0:T(8,128)(2,1)S(1)}, u32[]{:S(2)}, u32[]{:S(2)}) collective-permute-start(bf16[256,256]{1,0:T(8,128)(2,1)} %bitcast.13), channel_id=1, source_target_pairs={{0,1},{1,0},{2,3},{3,2},{4,5},{5,4},{6,7},{7,6},{8,9},{9,8},{10,11... | collective-permute-start | bytes 393224 | tf_op jit(solution)/shard_map/ppermute | solution.py:366
  7.4 2.1 %shard_map.84 = (f32[256,256]{1,0:T(8,128)S(1)}, bf16[256,256]{1,0:T(8,128)(2,1)S(1)}, bf16[256,256]{1,0:T(8,128)(2,1)S(1)}, bf16[6912,256]{1,0:T(8,128)(2,1)S(1...) custom-call(bf16[256,256]{1,0:T(8,128)(2,1)} %bitcast.14, ...), custom_call_target="tpu_custom_call" | custom-call | flops 369098752 | bytes 5353472 | tf_op jit(solution)/shard_map/pallas_call | solution.py:272
  9.5 0.5 collective-permute-done.1.far
  10.1 0.7 %shard_map.85 = (bf16[256,256]{1,0:T(8,128)(2,1)S(1)}, f32[256,256]{1,0:T(8,128)S(1)}, f32[256,256]{1,0:T(8,128)S(1)}, bf16[256,256]{1,0:T(8,128)(2,1)S(1)}) custom-call(bf16[256,256]{1,0:T(8,128)(2,1)S(1)} %collective-permute-done.1.far, bf16[256,256]{1,0:T(8,128)(2,1)S(1)} %get-tuple-element.26.w_in, bf16[6912,256]{1,0:T(8,128)(2,1)S(1)} %get-tuple-element.27.wd, ...), custom_call_target="tpu_custom_call" | custom-call | flops 335544320 | bytes 4849664 | tf_op jit(solution)/shard_map/pallas_call | solution.py:272
  10.8 1.5 %collective-permute-done.near = bf16[256,256]{1,0:T(8,128)(2,1)S(1)} collective-permute-done((bf16[256,256]{1,0:T(8,128)(2,1)}, bf16[256,256]{1,0:T(8,128)(2,1)S(1)}, u32[]{:S(2)}, u32[]{:S(2)}) %collective-permute-start) | collective-permute-done | bytes 131104 | tf_op jit(solution)/shard_map/ppermute | solution.py:366
  12.3 4.1 %shard_map.86 = (bf16[256,256]{1,0:T(8,128)(2,1)S(1)}, bf16[256,256]{1,0:T(8,128)(2,1)S(1)}, bf16[256,256]{1,0:T(8,128)(2,1)S(1)}, bf16[32,8,768]{2,1,0:T(8,128)(2,1)}) custom-call(bf16[256,256]{1,0:T(8,128)(2,1)S(1)} %collective-permute-done.near, bf16[256,256]{1,0:T(8,128)(2,1)S(1)} %get-tuple-element.29.far_t, bf16[256,256]{1,0:T(8,128)(2,1)S(1)} %get-tuple-element.30.xt, ...), custom_call_target="tpu_custom_call" | custom-call | flops 2348810240 | bytes 6160384 | tf_op jit(solution)/shard_map/pallas_call | solution.py:272
  16.3 8.4 %all-to-all-start = ((bf16[32,8,768]{2,1,0:T(8,128)(2,1)}), bf16[32,8,768]{2,1,0:T(8,128)(2,1)S(1)}, u32[]{:S(2)}, u32[]{:S(2)}) async-start(bf16[32,8,768]{2,1,0:T(8,128)(2,1)} %get-tuple-element.38), calls=%async_computation | async-start | bytes 786432 | tf_op jit(solution)/shard_map/all_to_all | solution.py:388
  24.8 0.3 shard_map.89
  25.0 1.3 %collective-permute-start.3 = (bf16[256,256]{1,0:T(8,128)(2,1)S(1)}, bf16[256,256]{1,0:T(8,128)(2,1)S(1)}, u32[]{:S(2)}, u32[]{:S(2)}) collective-permute-start(bf16[256,256]{1,0:T(8,128)(2,1)S(1)} %get-tuple-element.42), channel_id=1, source_target_pairs={{32,1},{33,0},{34,3},{35,2},{36,5},{37,4},{38,7},{39,6},{40,9},{41... | collective-permute-start | bytes 393224 | tf_op jit(solution)/shard_map/ppermute | solution.py:366
  26.3 0.2 shard_map.88
  26.6 1.3 %collective-permute-start.4 = (bf16[256,256]{1,0:T(8,128)(2,1)S(1)}, bf16[256,256]{1,0:T(8,128)(2,1)S(1)}, u32[]{:S(2)}, u32[]{:S(2)}) collective-permute-start(bf16[256,256]{1,0:T(8,128)(2,1)S(1)} %get-tuple-element.43), channel_id=1, source_target_pairs={{33,2},{34,1},{35,4},{36,3},{37,6},{38,5},{39,8},{40,7},{41,10},{4... | collective-permute-start | bytes 393224 | tf_op jit(solution)/shard_map/ppermute | solution.py:366
  27.9 1.3 %collective-permute-start.2 = (bf16[256,256]{1,0:T(8,128)(2,1)S(1)}, bf16[256,256]{1,0:T(8,128)(2,1)S(1)}, u32[]{:S(2)}, u32[]{:S(2)}) collective-permute-start(bf16[256,256]{1,0:T(8,128)(2,1)S(1)} %shard_map.88), channel_id=1, source_target_pairs={{32,0},{33,1},{34,2},{35,3},{36,4},{37,5},{38,6},{39,7},{40,8},{41... | collective-permute-start | bytes 393224 | tf_op jit(solution)/shard_map/ppermute | solution.py:366
  29.2 9.5 %all-to-all-done.got = bf16[32,8,768]{2,1,0:T(8,128)(2,1)S(1)} async-done(((bf16[32,8,768]{2,1,0:T(8,128)(2,1)}), bf16[32,8,768]{2,1,0:T(8,128)(2,1)S(1)}, u32[]{:S(2)}, u32[]{:S(2)}) %all-to-all-start) | async-done | bytes 393248 | tf_op jit(solution)/shard_map/all_to_all | solution.py:388
  38.7 0.7 %shard_map.87 = f32[4,8,384]{2,1,0:T(8,128)} custom-call(bf16[32,8,768]{2,1,0:T(8,128)(2,1)S(1)} %all-to-all-done.got), custom_call_target="tpu_custom_call" | custom-call | flops 1000 | bytes 442368 | tf_op jit(solution)/shard_map/pallas_call | solution.py:272
  39.4 10.3 %all-to-all-start.1 = ((f32[4,8,384]{2,1,0:T(8,128)}), f32[4,8,384]{2,1,0:T(8,128)S(1)}, u32[]{:S(2)}, u32[]{:S(2)}) async-start(f32[4,8,384]{2,1,0:T(8,128)} %shard_map.87), calls=%async_computation.1 | async-start | bytes 98304 | tf_op jit(solution)/shard_map/all_to_all | solution.py:389
  49.7 0.0 collective-permute-done.3.dxl
  49.7 0.0 collective-permute-done.4.dxr
  49.7 0.0 collective-permute-done.2.dx
  49.7 8.1 %all-to-all-done.1.got = f32[4,8,384]{2,1,0:T(8,128)S(1)} async-done(((f32[4,8,384]{2,1,0:T(8,128)}), f32[4,8,384]{2,1,0:T(8,128)S(1)}, u32[]{:S(2)}, u32[]{:S(2)}) %all-to-all-start.1) | async-done | bytes 49184 | tf_op jit(solution)/shard_map/all_to_all | solution.py:389
  57.8 0.8 %shard_map.90 = (f32[2,256]{1,0:T(2,128)}, f32[2,256]{1,0:T(2,128)}, f32[216,8]{1,0:T(8,128)}, bf16[256,256]{1,0:T(8,128)(2,1)}) custom-call(f32[4,8,384]{2,1,0:T(8,128)S(1)} %all-to-all-done.1.got, bf16[256,256]{1,0:T(8,128)(2,1)S(1)} %collective-permute-done.2.dx, bf16[256,256]{1,0:T(8,128)(2,1)S(1)} %collective-permute-done.3.dxl, ...), custom_call_target="tpu_custom_call" | custom-call | flops 1000 | bytes 584448 | tf_op jit(solution)/shard_map/pallas_call | solution.py:272
Async XLA Ops:
  0.6 9.4 %collective-permute-start.1 = (bf16[256,256]{1,0:T(8,128)(2,1)}, bf16[256,256]{1,0:T(8,128)(2,1)S(1)}, u32[]{:S(2)}, u32[]{:S(2)}) collective-permute-start(bf16[256,256]{1,0:T(8,128)(2,1)} %bitcast.12), channel_id=1, source_target_pairs={{1,2},{2,1},{3,4},{4,3},{5,6},{6,5},{7,8},{8,7},{9,10},{10,9},{11,... | collective-permute-start | bytes 393224 | tf_op jit(solution)/shard_map/ppermute | solution.py:366
  5.2 7.1 %collective-permute-start = (bf16[256,256]{1,0:T(8,128)(2,1)}, bf16[256,256]{1,0:T(8,128)(2,1)S(1)}, u32[]{:S(2)}, u32[]{:S(2)}) collective-permute-start(bf16[256,256]{1,0:T(8,128)(2,1)} %bitcast.13), channel_id=1, source_target_pairs={{0,1},{1,0},{2,3},{3,2},{4,5},{5,4},{6,7},{7,6},{8,9},{9,8},{10,11... | collective-permute-start | bytes 393224 | tf_op jit(solution)/shard_map/ppermute | solution.py:366
  16.3 22.3 %all-to-all-start = ((bf16[32,8,768]{2,1,0:T(8,128)(2,1)}), bf16[32,8,768]{2,1,0:T(8,128)(2,1)S(1)}, u32[]{:S(2)}, u32[]{:S(2)}) async-start(bf16[32,8,768]{2,1,0:T(8,128)(2,1)} %get-tuple-element.38), calls=%async_computation | async-start | bytes 786432 | tf_op jit(solution)/shard_map/all_to_all | solution.py:388
  25.0 24.6 %collective-permute-start.3 = (bf16[256,256]{1,0:T(8,128)(2,1)S(1)}, bf16[256,256]{1,0:T(8,128)(2,1)S(1)}, u32[]{:S(2)}, u32[]{:S(2)}) collective-permute-start(bf16[256,256]{1,0:T(8,128)(2,1)S(1)} %get-tuple-element.42), channel_id=1, source_target_pairs={{32,1},{33,0},{34,3},{35,2},{36,5},{37,4},{38,7},{39,6},{40,9},{41... | collective-permute-start | bytes 393224 | tf_op jit(solution)/shard_map/ppermute | solution.py:366
  26.6 23.1 %collective-permute-start.4 = (bf16[256,256]{1,0:T(8,128)(2,1)S(1)}, bf16[256,256]{1,0:T(8,128)(2,1)S(1)}, u32[]{:S(2)}, u32[]{:S(2)}) collective-permute-start(bf16[256,256]{1,0:T(8,128)(2,1)S(1)} %get-tuple-element.43), channel_id=1, source_target_pairs={{33,2},{34,1},{35,4},{36,3},{37,6},{38,5},{39,8},{40,7},{41,10},{4... | collective-permute-start | bytes 393224 | tf_op jit(solution)/shard_map/ppermute | solution.py:366
  27.9 21.8 %collective-permute-start.2 = (bf16[256,256]{1,0:T(8,128)(2,1)S(1)}, bf16[256,256]{1,0:T(8,128)(2,1)S(1)}, u32[]{:S(2)}, u32[]{:S(2)}) collective-permute-start(bf16[256,256]{1,0:T(8,128)(2,1)S(1)} %shard_map.88), channel_id=1, source_target_pairs={{32,0},{33,1},{34,2},{35,3},{36,4},{37,5},{38,6},{39,7},{40,8},{41... | collective-permute-start | bytes 393224 | tf_op jit(solution)/shard_map/ppermute | solution.py:366
  39.4 18.4 %all-to-all-start.1 = ((f32[4,8,384]{2,1,0:T(8,128)}), f32[4,8,384]{2,1,0:T(8,128)S(1)}, u32[]{:S(2)}, u32[]{:S(2)}) async-start(f32[4,8,384]{2,1,0:T(8,128)} %shard_map.87), calls=%async_computation.1 | async-start | bytes 98304 | tf_op jit(solution)/shard_map/all_to_all | solution.py:389

commit v6 on v5

--- a/solution.py
+++ b/solution.py
@@ -18,6 +18,8 @@
 PAD_ROWS = CELLS + 2 * SIDE
 NDEV = 128
 INTERPRET = False
+SAMPLE_ORDER = [3, 2, 1, 0]
+ORDER = list(range(C // GW - 1, -1, -1))
 
 NT = (((1,), (1,)), ((), ()))
 
@@ -228,9 +230,10 @@
     blocks = C // GW
     packed = pack[...].reshape(NDEV, 8, half).astype(BF16)
     gg = taps[...].T.reshape(blocks, GW, C).astype(BF16)
-    for part in range(NDEV // blocks):
-        pay[:, :, part * half : (part + 1) * half] = packed[part * blocks : (part + 1) * blocks]
-    pay[:, :, 4 * half :] = gg
+    for at, plane in enumerate(ORDER):
+        for part in range(NDEV // blocks):
+            pay[at, :, part * half : (part + 1) * half] = packed[part * blocks + plane]
+        pay[at, :, 4 * half :] = gg[plane]
 
 
 def own_dx_kernel(own, cot, w_in, dx):
@@ -245,9 +248,9 @@
 def first_sum_kernel(got, pay):
     total = jnp.sum(got[...].astype(F32), axis=0)
     half = C // 2
-    for part in range(4):
-        pay[part, :, 0:half] = total[:, part * half : (part + 1) * half]
-        pay[part, :, half:] = total[:, 4 * half :]
+    for at, part in enumerate(SAMPLE_ORDER):
+        pay[at, :, 0:half] = total[:, part * half : (part + 1) * half]
+        pay[at, :, half:] = total[:, 4 * half :]
 
 
 def sum_kernel(got, dx, dxl, dxr, grad_in, grad_out, gg, section):
@@ -385,8 +388,10 @@
         near, far_t, xt, cot, w_in, wd, z2f, dh2, h1t, slope1, h1ft, slopef
     )
     dx = own_dx_stage(own, cot, w_in)
-    part = first_sum_stage(lax.all_to_all(pay, "sg", 0, 0, tiled=True))
-    got = lax.all_to_all(part, "dp", 0, 0, tiled=True)
+    part = first_sum_stage(lax.all_to_all(pay, "sg", 0, 0, tiled=True, axis_index_groups=[ORDER]))
+    got = lax.all_to_all(
+        part, "dp", 0, 0, tiled=True, axis_index_groups=[SAMPLE_ORDER]
+    )
     dx_near, dx_far = pair_dx_stage(to_near, to_far, w_in)
     dx = sent(dx, 1, lambda plane: plane)
     dx_far = sent(dx_far, 1, far_of)

time: 59.3 us -> 55.8 us (0.941)
  waiting for transfers between devices: 19.7 us -> 12.8 us
  starting transfers between devices: 29.4 us -> 32.9 us
    all_to_all x2, waiting for transfers between devices: 17.6 us -> 10.8 us  [the longest x1 6.3 us: per_device(): lax.all_to_all(pay, 'sg', 0, 0, tiled=True, axis_index_groups=[ORDER])]
    all_to_all x2, starting transfers between devices: 18.7 us -> 22.3 us  [the longest x1 12.3 us: per_device(): lax.all_to_all(part, 'dp', 0, 0, tiled=True, axis_index_groups=[SAMPLE_OR...]
where the time goes in v6:
time: 55.8 us; the launch traced here: 55.3 us
  starting transfers between devices  32.9 us (59%)
  waiting for transfers between devices  12.8 us (23%)
  Pallas kernels  8.83 us (16%)
  between operations  0.72 us (1%)
    all_to_all x1, starting transfers between devices, per_device(): lax.all_to_all(part, 'dp', 0, 0, tiled=True, axis_index_groups=[SAMPLE_OR...  12.3 us
    ppermute x5, starting transfers between devices, sent(): return lax.ppermute(value, ('pipe', 'sg'), pairs)  10.7 us
    all_to_all x1, starting transfers between devices, per_device(): lax.all_to_all(pay, 'sg', 0, 0, tiled=True, axis_index_groups=[ORDER])  9.99 us
    pallas_call x7, Pallas kernels, call(): pl.pallas_call(kernel, out_shape=shapes, in_specs=[pl.BlockSpec(memory_sp...  8.83 us
    all_to_all x1, waiting for transfers between devices, per_device(): lax.all_to_all(pay, 'sg', 0, 0, tiled=True, axis_index_groups=[ORDER])  6.3 us
    all_to_all x1, waiting for transfers between devices, per_device(): lax.all_to_all(part, 'dp', 0, 0, tiled=True, axis_index_groups=[SAMPLE_OR...  4.47 us
    ppermute x5, waiting for transfers between devices, sent(): return lax.ppermute(value, ('pipe', 'sg'), pairs)  2.05 us
  transfers between devices with their start and end apart: 7, of which 4 were waited for; matrix products, arithmetic and copies ran while one was open for 0% of the time, Pallas kernels for 7%

profile of v6, /device:TPU:8, one launch (start us, length us, event | category | flops | bytes accessed | tf_op | source)
XLA Modules:
  0.0 55.3 jit_solution(14025517554674215107)
XLA Ops:
  0.6 4.6 %collective-permute-start.1 = (bf16[256,256]{1,0:T(8,128)(2,1)}, bf16[256,256]{1,0:T(8,128)(2,1)S(1)}, u32[]{:S(2)}, u32[]{:S(2)}) collective-permute-start(bf16[256,256]{1,0:T(8,128)(2,1)} %bitcast.12), channel_id=1, source_target_pairs={{1,2},{2,1},{3,4},{4,3},{5,6},{6,5},{7,8},{8,7},{9,10},{10,9},{11,... | collective-permute-start | bytes 393224 | tf_op jit(solution)/shard_map/ppermute | solution.py:369
  5.2 2.2 %collective-permute-start = (bf16[256,256]{1,0:T(8,128)(2,1)}, bf16[256,256]{1,0:T(8,128)(2,1)S(1)}, u32[]{:S(2)}, u32[]{:S(2)}) collective-permute-start(bf16[256,256]{1,0:T(8,128)(2,1)} %bitcast.13), channel_id=1, source_target_pairs={{0,1},{1,0},{2,3},{3,2},{4,5},{5,4},{6,7},{7,6},{8,9},{9,8},{10,11... | collective-permute-start | bytes 393224 | tf_op jit(solution)/shard_map/ppermute | solution.py:369
  7.4 2.1 %shard_map.84 = (f32[256,256]{1,0:T(8,128)S(1)}, bf16[256,256]{1,0:T(8,128)(2,1)S(1)}, bf16[256,256]{1,0:T(8,128)(2,1)S(1)}, bf16[6912,256]{1,0:T(8,128)(2,1)S(1...) custom-call(bf16[256,256]{1,0:T(8,128)(2,1)} %bitcast.14, ...), custom_call_target="tpu_custom_call" | custom-call | flops 369098752 | bytes 5353472 | tf_op jit(solution)/shard_map/pallas_call | solution.py:275
  9.5 0.5 collective-permute-done.1.far
  10.1 0.7 %shard_map.85 = (bf16[256,256]{1,0:T(8,128)(2,1)S(1)}, f32[256,256]{1,0:T(8,128)S(1)}, f32[256,256]{1,0:T(8,128)S(1)}, bf16[256,256]{1,0:T(8,128)(2,1)S(1)}) custom-call(bf16[256,256]{1,0:T(8,128)(2,1)S(1)} %collective-permute-done.1.far, bf16[256,256]{1,0:T(8,128)(2,1)S(1)} %get-tuple-element.26.w_in, bf16[6912,256]{1,0:T(8,128)(2,1)S(1)} %get-tuple-element.27.wd, ...), custom_call_target="tpu_custom_call" | custom-call | flops 335544320 | bytes 4849664 | tf_op jit(solution)/shard_map/pallas_call | solution.py:275
  10.8 1.5 %collective-permute-done.near = bf16[256,256]{1,0:T(8,128)(2,1)S(1)} collective-permute-done((bf16[256,256]{1,0:T(8,128)(2,1)}, bf16[256,256]{1,0:T(8,128)(2,1)S(1)}, u32[]{:S(2)}, u32[]{:S(2)}) %collective-permute-start) | collective-permute-done | bytes 131104 | tf_op jit(solution)/shard_map/ppermute | solution.py:369
  12.3 4.1 %shard_map.86 = (bf16[256,256]{1,0:T(8,128)(2,1)S(1)}, bf16[256,256]{1,0:T(8,128)(2,1)S(1)}, bf16[256,256]{1,0:T(8,128)(2,1)S(1)}, bf16[32,8,768]{2,1,0:T(8,128)(2,1)}) custom-call(bf16[256,256]{1,0:T(8,128)(2,1)S(1)} %collective-permute-done.near, bf16[256,256]{1,0:T(8,128)(2,1)S(1)} %get-tuple-element.29.far_t, bf16[256,256]{1,0:T(8,128)(2,1)S(1)} %get-tuple-element.30.xt, ...), custom_call_target="tpu_custom_call" | custom-call | flops 2348810240 | bytes 6160384 | tf_op jit(solution)/shard_map/pallas_call | solution.py:275
  16.3 10.0 %all-to-all-start = ((bf16[32,8,768]{2,1,0:T(8,128)(2,1)}), bf16[32,8,768]{2,1,0:T(8,128)(2,1)S(1)}, u32[]{:S(2)}, u32[]{:S(2)}) async-start(bf16[32,8,768]{2,1,0:T(8,128)(2,1)} %get-tuple-element.38), calls=%async_computation | async-start | bytes 786432 | tf_op jit(solution)/shard_map/all_to_all | solution.py:391
  26.3 0.3 shard_map.89
  26.6 1.3 %collective-permute-start.3 = (bf16[256,256]{1,0:T(8,128)(2,1)S(1)}, bf16[256,256]{1,0:T(8,128)(2,1)S(1)}, u32[]{:S(2)}, u32[]{:S(2)}) collective-permute-start(bf16[256,256]{1,0:T(8,128)(2,1)S(1)} %get-tuple-element.42), channel_id=1, source_target_pairs={{32,1},{33,0},{34,3},{35,2},{36,5},{37,4},{38,7},{39,6},{40,9},{41... | collective-permute-start | bytes 393224 | tf_op jit(solution)/shard_map/ppermute | solution.py:369
  27.9 0.2 shard_map.88
  28.1 1.3 %collective-permute-start.4 = (bf16[256,256]{1,0:T(8,128)(2,1)S(1)}, bf16[256,256]{1,0:T(8,128)(2,1)S(1)}, u32[]{:S(2)}, u32[]{:S(2)}) collective-permute-start(bf16[256,256]{1,0:T(8,128)(2,1)S(1)} %get-tuple-element.43), channel_id=1, source_target_pairs={{33,2},{34,1},{35,4},{36,3},{37,6},{38,5},{39,8},{40,7},{41,10},{4... | collective-permute-start | bytes 393224 | tf_op jit(solution)/shard_map/ppermute | solution.py:369
  29.4 1.3 %collective-permute-start.2 = (bf16[256,256]{1,0:T(8,128)(2,1)S(1)}, bf16[256,256]{1,0:T(8,128)(2,1)S(1)}, u32[]{:S(2)}, u32[]{:S(2)}) collective-permute-start(bf16[256,256]{1,0:T(8,128)(2,1)S(1)} %shard_map.88), channel_id=1, source_target_pairs={{32,0},{33,1},{34,2},{35,3},{36,4},{37,5},{38,6},{39,7},{40,8},{41... | collective-permute-start | bytes 393224 | tf_op jit(solution)/shard_map/ppermute | solution.py:369
  30.7 6.3 %all-to-all-done.got = bf16[32,8,768]{2,1,0:T(8,128)(2,1)S(1)} async-done(((bf16[32,8,768]{2,1,0:T(8,128)(2,1)}), bf16[32,8,768]{2,1,0:T(8,128)(2,1)S(1)}, u32[]{:S(2)}, u32[]{:S(2)}) %all-to-all-start) | async-done | bytes 393248 | tf_op jit(solution)/shard_map/all_to_all | solution.py:391
  37.0 0.7 %shard_map.87 = f32[4,8,384]{2,1,0:T(8,128)} custom-call(bf16[32,8,768]{2,1,0:T(8,128)(2,1)S(1)} %all-to-all-done.got), custom_call_target="tpu_custom_call" | custom-call | flops 1000 | bytes 442368 | tf_op jit(solution)/shard_map/pallas_call | solution.py:275
  37.7 12.3 %all-to-all-start.1 = ((f32[4,8,384]{2,1,0:T(8,128)}), f32[4,8,384]{2,1,0:T(8,128)S(1)}, u32[]{:S(2)}, u32[]{:S(2)}) async-start(f32[4,8,384]{2,1,0:T(8,128)} %shard_map.87), calls=%async_computation.1 | async-start | bytes 98304 | tf_op jit(solution)/shard_map/all_to_all | solution.py:392
  50.0 0.0 collective-permute-done.3.dxl
  50.0 0.0 collective-permute-done.4.dxr
  50.0 0.0 collective-permute-done.2.dx
  50.0 4.5 %all-to-all-done.1.got = f32[4,8,384]{2,1,0:T(8,128)S(1)} async-done(((f32[4,8,384]{2,1,0:T(8,128)}), f32[4,8,384]{2,1,0:T(8,128)S(1)}, u32[]{:S(2)}, u32[]{:S(2)}) %all-to-all-start.1) | async-done | bytes 49184 | tf_op jit(solution)/shard_map/all_to_all | solution.py:392
  54.5 0.8 %shard_map.90 = (f32[2,256]{1,0:T(2,128)}, f32[2,256]{1,0:T(2,128)}, f32[216,8]{1,0:T(8,128)}, bf16[256,256]{1,0:T(8,128)(2,1)}) custom-call(f32[4,8,384]{2,1,0:T(8,128)S(1)} %all-to-all-done.1.got, bf16[256,256]{1,0:T(8,128)(2,1)S(1)} %collective-permute-done.2.dx, bf16[256,256]{1,0:T(8,128)(2,1)S(1)} %collective-permute-done.3.dxl, ...), custom_call_target="tpu_custom_call" | custom-call | flops 1000 | bytes 584448 | tf_op jit(solution)/shard_map/pallas_call | solution.py:275
Async XLA Ops:
  0.6 9.4 %collective-permute-start.1 = (bf16[256,256]{1,0:T(8,128)(2,1)}, bf16[256,256]{1,0:T(8,128)(2,1)S(1)}, u32[]{:S(2)}, u32[]{:S(2)}) collective-permute-start(bf16[256,256]{1,0:T(8,128)(2,1)} %bitcast.12), channel_id=1, source_target_pairs={{1,2},{2,1},{3,4},{4,3},{5,6},{6,5},{7,8},{8,7},{9,10},{10,9},{11,... | collective-permute-start | bytes 393224 | tf_op jit(solution)/shard_map/ppermute | solution.py:369
  5.2 7.1 %collective-permute-start = (bf16[256,256]{1,0:T(8,128)(2,1)}, bf16[256,256]{1,0:T(8,128)(2,1)S(1)}, u32[]{:S(2)}, u32[]{:S(2)}) collective-permute-start(bf16[256,256]{1,0:T(8,128)(2,1)} %bitcast.13), channel_id=1, source_target_pairs={{0,1},{1,0},{2,3},{3,2},{4,5},{5,4},{6,7},{7,6},{8,9},{9,8},{10,11... | collective-permute-start | bytes 393224 | tf_op jit(solution)/shard_map/ppermute | solution.py:369
  16.3 20.7 %all-to-all-start = ((bf16[32,8,768]{2,1,0:T(8,128)(2,1)}), bf16[32,8,768]{2,1,0:T(8,128)(2,1)S(1)}, u32[]{:S(2)}, u32[]{:S(2)}) async-start(bf16[32,8,768]{2,1,0:T(8,128)(2,1)} %get-tuple-element.38), calls=%async_computation | async-start | bytes 786432 | tf_op jit(solution)/shard_map/all_to_all | solution.py:391
  26.6 23.4 %collective-permute-start.3 = (bf16[256,256]{1,0:T(8,128)(2,1)S(1)}, bf16[256,256]{1,0:T(8,128)(2,1)S(1)}, u32[]{:S(2)}, u32[]{:S(2)}) collective-permute-start(bf16[256,256]{1,0:T(8,128)(2,1)S(1)} %get-tuple-element.42), channel_id=1, source_target_pairs={{32,1},{33,0},{34,3},{35,2},{36,5},{37,4},{38,7},{39,6},{40,9},{41... | collective-permute-start | bytes 393224 | tf_op jit(solution)/shard_map/ppermute | solution.py:369
  28.1 21.9 %collective-permute-start.4 = (bf16[256,256]{1,0:T(8,128)(2,1)S(1)}, bf16[256,256]{1,0:T(8,128)(2,1)S(1)}, u32[]{:S(2)}, u32[]{:S(2)}) collective-permute-start(bf16[256,256]{1,0:T(8,128)(2,1)S(1)} %get-tuple-element.43), channel_id=1, source_target_pairs={{33,2},{34,1},{35,4},{36,3},{37,6},{38,5},{39,8},{40,7},{41,10},{4... | collective-permute-start | bytes 393224 | tf_op jit(solution)/shard_map/ppermute | solution.py:369
  29.4 20.6 %collective-permute-start.2 = (bf16[256,256]{1,0:T(8,128)(2,1)S(1)}, bf16[256,256]{1,0:T(8,128)(2,1)S(1)}, u32[]{:S(2)}, u32[]{:S(2)}) collective-permute-start(bf16[256,256]{1,0:T(8,128)(2,1)S(1)} %shard_map.88), channel_id=1, source_target_pairs={{32,0},{33,1},{34,2},{35,3},{36,4},{37,5},{38,6},{39,7},{40,8},{41... | collective-permute-start | bytes 393224 | tf_op jit(solution)/shard_map/ppermute | solution.py:369
  37.7 16.8 %all-to-all-start.1 = ((f32[4,8,384]{2,1,0:T(8,128)}), f32[4,8,384]{2,1,0:T(8,128)S(1)}, u32[]{:S(2)}, u32[]{:S(2)}) async-start(f32[4,8,384]{2,1,0:T(8,128)} %shard_map.87), calls=%async_computation.1 | async-start | bytes 98304 | tf_op jit(solution)/shard_map/all_to_all | solution.py:392

commit v7 on v6

--- a/solution.py
+++ b/solution.py
@@ -18,8 +18,8 @@
 PAD_ROWS = CELLS + 2 * SIDE
 NDEV = 128
 INTERPRET = False
-SAMPLE_ORDER = [3, 2, 1, 0]
-ORDER = list(range(C // GW - 1, -1, -1))
+SAMPLE_ORDER = [2, 3, 0, 1]
+ORDER = [(20 - step) % (C // GW) for step in range(C // GW)]
 
 NT = (((1,), (1,)), ((), ()))
 

time: 55.8 us -> 53.8 us (0.964)
  the two profiles are of different devices: /device:TPU:8 before, /device:TPU:2 now
where the time goes in v7:
time: 53.8 us; the launch traced here: 53.4 us
  starting transfers between devices  34.8 us (65%)
  waiting for transfers between devices  8.97 us (17%)
  Pallas kernels  8.84 us (16%)
  between operations  0.72 us (1%)
    all_to_all x1, starting transfers between devices, per_device(): lax.all_to_all(part, 'dp', 0, 0, tiled=True, axis_index_groups=[SAMPLE_OR...  12.5 us
    ppermute x5, starting transfers between devices, sent(): return lax.ppermute(value, ('pipe', 'sg'), pairs)  12.4 us
    all_to_all x1, starting transfers between devices, per_device(): lax.all_to_all(pay, 'sg', 0, 0, tiled=True, axis_index_groups=[ORDER])  9.93 us
    pallas_call x7, Pallas kernels, call(): pl.pallas_call(kernel, out_shape=shapes, in_specs=[pl.BlockSpec(memory_sp...  8.84 us
    all_to_all x1, waiting for transfers between devices, per_device(): lax.all_to_all(pay, 'sg', 0, 0, tiled=True, axis_index_groups=[ORDER])  6.07 us
    all_to_all x1, waiting for transfers between devices, per_device(): lax.all_to_all(part, 'dp', 0, 0, tiled=True, axis_index_groups=[SAMPLE_OR...  2.54 us
  transfers between devices with their start and end apart: 7, of which 3 were waited for; matrix products, arithmetic and copies ran while one was open for 0% of the time, Pallas kernels for 7%

profile of v7, /device:TPU:2, one launch (start us, length us, event | category | flops | bytes accessed | tf_op | source)
XLA Modules:
  0.0 53.4 jit_solution(3211564508233697877)
XLA Ops:
  0.6 3.4 %collective-permute-start.1 = (bf16[256,256]{1,0:T(8,128)(2,1)}, bf16[256,256]{1,0:T(8,128)(2,1)S(1)}, u32[]{:S(2)}, u32[]{:S(2)}) collective-permute-start(bf16[256,256]{1,0:T(8,128)(2,1)} %bitcast.12), channel_id=1, source_target_pairs={{1,2},{2,1},{3,4},{4,3},{5,6},{6,5},{7,8},{8,7},{9,10},{10,9},{11,... | collective-permute-start | bytes 393224 | tf_op jit(solution)/shard_map/ppermute | solution.py:369
  4.0 5.1 %collective-permute-start = (bf16[256,256]{1,0:T(8,128)(2,1)}, bf16[256,256]{1,0:T(8,128)(2,1)S(1)}, u32[]{:S(2)}, u32[]{:S(2)}) collective-permute-start(bf16[256,256]{1,0:T(8,128)(2,1)} %bitcast.13), channel_id=1, source_target_pairs={{0,1},{1,0},{2,3},{3,2},{4,5},{5,4},{6,7},{7,6},{8,9},{9,8},{10,11... | collective-permute-start | bytes 393224 | tf_op jit(solution)/shard_map/ppermute | solution.py:369
  9.1 2.1 %shard_map.84 = (f32[256,256]{1,0:T(8,128)S(1)}, bf16[256,256]{1,0:T(8,128)(2,1)S(1)}, bf16[256,256]{1,0:T(8,128)(2,1)S(1)}, bf16[6912,256]{1,0:T(8,128)(2,1)S(1...) custom-call(bf16[256,256]{1,0:T(8,128)(2,1)} %bitcast.14, ...), custom_call_target="tpu_custom_call" | custom-call | flops 369098752 | bytes 5353472 | tf_op jit(solution)/shard_map/pallas_call | solution.py:275
  11.2 0.0 collective-permute-done.1.far
  11.2 0.7 %shard_map.85 = (bf16[256,256]{1,0:T(8,128)(2,1)S(1)}, f32[256,256]{1,0:T(8,128)S(1)}, f32[256,256]{1,0:T(8,128)S(1)}, bf16[256,256]{1,0:T(8,128)(2,1)S(1)}) custom-call(bf16[256,256]{1,0:T(8,128)(2,1)S(1)} %collective-permute-done.1.far, bf16[256,256]{1,0:T(8,128)(2,1)S(1)} %get-tuple-element.26.w_in, bf16[6912,256]{1,0:T(8,128)(2,1)S(1)} %get-tuple-element.27.wd, ...), custom_call_target="tpu_custom_call" | custom-call | flops 335544320 | bytes 4849664 | tf_op jit(solution)/shard_map/pallas_call | solution.py:275
  11.9 0.4 collective-permute-done.near
  12.3 4.1 %shard_map.86 = (bf16[256,256]{1,0:T(8,128)(2,1)S(1)}, bf16[256,256]{1,0:T(8,128)(2,1)S(1)}, bf16[256,256]{1,0:T(8,128)(2,1)S(1)}, bf16[32,8,768]{2,1,0:T(8,128)(2,1)}) custom-call(bf16[256,256]{1,0:T(8,128)(2,1)S(1)} %collective-permute-done.near, bf16[256,256]{1,0:T(8,128)(2,1)S(1)} %get-tuple-element.29.far_t, bf16[256,256]{1,0:T(8,128)(2,1)S(1)} %get-tuple-element.30.xt, ...), custom_call_target="tpu_custom_call" | custom-call | flops 2348810240 | bytes 6160384 | tf_op jit(solution)/shard_map/pallas_call | solution.py:275
  16.4 9.9 %all-to-all-start = ((bf16[32,8,768]{2,1,0:T(8,128)(2,1)}), bf16[32,8,768]{2,1,0:T(8,128)(2,1)S(1)}, u32[]{:S(2)}, u32[]{:S(2)}) async-start(bf16[32,8,768]{2,1,0:T(8,128)(2,1)} %get-tuple-element.38), calls=%async_computation | async-start | bytes 786432 | tf_op jit(solution)/shard_map/all_to_all | solution.py:391
  26.3 0.3 shard_map.89
  26.6 1.3 %collective-permute-start.3 = (bf16[256,256]{1,0:T(8,128)(2,1)S(1)}, bf16[256,256]{1,0:T(8,128)(2,1)S(1)}, u32[]{:S(2)}, u32[]{:S(2)}) collective-permute-start(bf16[256,256]{1,0:T(8,128)(2,1)S(1)} %get-tuple-element.42), channel_id=1, source_target_pairs={{32,1},{33,0},{34,3},{35,2},{36,5},{37,4},{38,7},{39,6},{40,9},{41... | collective-permute-start | bytes 393224 | tf_op jit(solution)/shard_map/ppermute | solution.py:369
  27.9 0.2 shard_map.88
  28.1 1.3 %collective-permute-start.4 = (bf16[256,256]{1,0:T(8,128)(2,1)S(1)}, bf16[256,256]{1,0:T(8,128)(2,1)S(1)}, u32[]{:S(2)}, u32[]{:S(2)}) collective-permute-start(bf16[256,256]{1,0:T(8,128)(2,1)S(1)} %get-tuple-element.43), channel_id=1, source_target_pairs={{33,2},{34,1},{35,4},{36,3},{37,6},{38,5},{39,8},{40,7},{41,10},{4... | collective-permute-start | bytes 393224 | tf_op jit(solution)/shard_map/ppermute | solution.py:369
  29.4 1.3 %collective-permute-start.2 = (bf16[256,256]{1,0:T(8,128)(2,1)S(1)}, bf16[256,256]{1,0:T(8,128)(2,1)S(1)}, u32[]{:S(2)}, u32[]{:S(2)}) collective-permute-start(bf16[256,256]{1,0:T(8,128)(2,1)S(1)} %shard_map.88), channel_id=1, source_target_pairs={{32,0},{33,1},{34,2},{35,3},{36,4},{37,5},{38,6},{39,7},{40,8},{41... | collective-permute-start | bytes 393224 | tf_op jit(solution)/shard_map/ppermute | solution.py:369
  30.7 6.1 %all-to-all-done.got = bf16[32,8,768]{2,1,0:T(8,128)(2,1)S(1)} async-done(((bf16[32,8,768]{2,1,0:T(8,128)(2,1)}), bf16[32,8,768]{2,1,0:T(8,128)(2,1)S(1)}, u32[]{:S(2)}, u32[]{:S(2)}) %all-to-all-start) | async-done | bytes 393248 | tf_op jit(solution)/shard_map/all_to_all | solution.py:391
  36.8 0.7 %shard_map.87 = f32[4,8,384]{2,1,0:T(8,128)} custom-call(bf16[32,8,768]{2,1,0:T(8,128)(2,1)S(1)} %all-to-all-done.got), custom_call_target="tpu_custom_call" | custom-call | flops 1000 | bytes 442368 | tf_op jit(solution)/shard_map/pallas_call | solution.py:275
  37.4 12.5 %all-to-all-start.1 = ((f32[4,8,384]{2,1,0:T(8,128)}), f32[4,8,384]{2,1,0:T(8,128)S(1)}, u32[]{:S(2)}, u32[]{:S(2)}) async-start(f32[4,8,384]{2,1,0:T(8,128)} %shard_map.87), calls=%async_computation.1 | async-start | bytes 98304 | tf_op jit(solution)/shard_map/all_to_all | solution.py:392
  50.0 0.0 collective-permute-done.3.dxl
  50.0 0.0 collective-permute-done.4.dxr
  50.0 0.0 collective-permute-done.2.dx
  50.0 2.5 %all-to-all-done.1.got = f32[4,8,384]{2,1,0:T(8,128)S(1)} async-done(((f32[4,8,384]{2,1,0:T(8,128)}), f32[4,8,384]{2,1,0:T(8,128)S(1)}, u32[]{:S(2)}, u32[]{:S(2)}) %all-to-all-start.1) | async-done | bytes 49184 | tf_op jit(solution)/shard_map/all_to_all | solution.py:392
  52.5 0.8 %shard_map.90 = (f32[2,256]{1,0:T(2,128)}, f32[2,256]{1,0:T(2,128)}, f32[216,8]{1,0:T(8,128)}, bf16[256,256]{1,0:T(8,128)(2,1)}) custom-call(f32[4,8,384]{2,1,0:T(8,128)S(1)} %all-to-all-done.1.got, bf16[256,256]{1,0:T(8,128)(2,1)S(1)} %collective-permute-done.2.dx, bf16[256,256]{1,0:T(8,128)(2,1)S(1)} %collective-permute-done.3.dxl, ...), custom_call_target="tpu_custom_call" | custom-call | flops 1000 | bytes 584448 | tf_op jit(solution)/shard_map/pallas_call | solution.py:275
Async XLA Ops:
  0.6 10.6 %collective-permute-start.1 = (bf16[256,256]{1,0:T(8,128)(2,1)}, bf16[256,256]{1,0:T(8,128)(2,1)S(1)}, u32[]{:S(2)}, u32[]{:S(2)}) collective-permute-start(bf16[256,256]{1,0:T(8,128)(2,1)} %bitcast.12), channel_id=1, source_target_pairs={{1,2},{2,1},{3,4},{4,3},{5,6},{6,5},{7,8},{8,7},{9,10},{10,9},{11,... | collective-permute-start | bytes 393224 | tf_op jit(solution)/shard_map/ppermute | solution.py:369
  4.0 8.2 %collective-permute-start = (bf16[256,256]{1,0:T(8,128)(2,1)}, bf16[256,256]{1,0:T(8,128)(2,1)S(1)}, u32[]{:S(2)}, u32[]{:S(2)}) collective-permute-start(bf16[256,256]{1,0:T(8,128)(2,1)} %bitcast.13), channel_id=1, source_target_pairs={{0,1},{1,0},{2,3},{3,2},{4,5},{5,4},{6,7},{7,6},{8,9},{9,8},{10,11... | collective-permute-start | bytes 393224 | tf_op jit(solution)/shard_map/ppermute | solution.py:369
  16.4 20.4 %all-to-all-start = ((bf16[32,8,768]{2,1,0:T(8,128)(2,1)}), bf16[32,8,768]{2,1,0:T(8,128)(2,1)S(1)}, u32[]{:S(2)}, u32[]{:S(2)}) async-start(bf16[32,8,768]{2,1,0:T(8,128)(2,1)} %get-tuple-element.38), calls=%async_computation | async-start | bytes 786432 | tf_op jit(solution)/shard_map/all_to_all | solution.py:391
  26.6 23.4 %collective-permute-start.3 = (bf16[256,256]{1,0:T(8,128)(2,1)S(1)}, bf16[256,256]{1,0:T(8,128)(2,1)S(1)}, u32[]{:S(2)}, u32[]{:S(2)}) collective-permute-start(bf16[256,256]{1,0:T(8,128)(2,1)S(1)} %get-tuple-element.42), channel_id=1, source_target_pairs={{32,1},{33,0},{34,3},{35,2},{36,5},{37,4},{38,7},{39,6},{40,9},{41... | collective-permute-start | bytes 393224 | tf_op jit(solution)/shard_map/ppermute | solution.py:369
  28.1 21.9 %collective-permute-start.4 = (bf16[256,256]{1,0:T(8,128)(2,1)S(1)}, bf16[256,256]{1,0:T(8,128)(2,1)S(1)}, u32[]{:S(2)}, u32[]{:S(2)}) collective-permute-start(bf16[256,256]{1,0:T(8,128)(2,1)S(1)} %get-tuple-element.43), channel_id=1, source_target_pairs={{33,2},{34,1},{35,4},{36,3},{37,6},{38,5},{39,8},{40,7},{41,10},{4... | collective-permute-start | bytes 393224 | tf_op jit(solution)/shard_map/ppermute | solution.py:369
  29.4 20.6 %collective-permute-start.2 = (bf16[256,256]{1,0:T(8,128)(2,1)S(1)}, bf16[256,256]{1,0:T(8,128)(2,1)S(1)}, u32[]{:S(2)}, u32[]{:S(2)}) collective-permute-start(bf16[256,256]{1,0:T(8,128)(2,1)S(1)} %shard_map.88), channel_id=1, source_target_pairs={{32,0},{33,1},{34,2},{35,3},{36,4},{37,5},{38,6},{39,7},{40,8},{41... | collective-permute-start | bytes 393224 | tf_op jit(solution)/shard_map/ppermute | solution.py:369
  37.4 15.1 %all-to-all-start.1 = ((f32[4,8,384]{2,1,0:T(8,128)}), f32[4,8,384]{2,1,0:T(8,128)S(1)}, u32[]{:S(2)}, u32[]{:S(2)}) async-start(f32[4,8,384]{2,1,0:T(8,128)} %shard_map.87), calls=%async_computation.1 | async-start | bytes 98304 | tf_op jit(solution)/shard_map/all_to_all | solution.py:392

commit v8 on v7

--- a/solution.py
+++ b/solution.py
@@ -253,10 +253,13 @@
         pay[at, :, half:] = total[:, 4 * half :]
 
 
-def sum_kernel(got, dx, dxl, dxr, grad_in, grad_out, gg, section):
+def section_kernel(dx, dx_near, dx_far, section):
     section[...] = (
-        dx[...].astype(F32) + (dxl[...].astype(F32) + dxr[...].astype(F32))
+        dx[...].astype(F32) + (dx_near[...].astype(F32) + dx_far[...].astype(F32))
     ).astype(BF16)
+
+
+def sum_kernel(got, grad_in, grad_out, gg):
     total = jnp.sum(got[...].astype(F32), axis=0)
     half = C // 2
     for which, out in enumerate((grad_in, grad_out)):
@@ -340,10 +343,14 @@
     return call(first_sum_kernel, [((4, 8, 3 * C // 2), F32)], [], 1000, got)[0]
 
 
+def section_stage(*args):
+    return call(section_kernel, [(PLANE, BF16)], [], 1000, *args)[0]
+
+
 def sum_stage(*args):
     return call(
         sum_kernel,
-        [((2, C), F32), ((2, C), F32), ((TAPS * GW, GW), F32), (PLANE, BF16)],
+        [((2, C), F32), ((2, C), F32), ((TAPS * GW, GW), F32)],
         [],
         1000,
         *args,
@@ -396,7 +403,8 @@
     dx = sent(dx, 1, lambda plane: plane)
     dx_far = sent(dx_far, 1, far_of)
     dx_near = sent(dx_near, 1, near_of)
-    grad_in, grad_out, gg, section_grad = sum_stage(got, dx, dx_near, dx_far)
+    section_grad = section_stage(dx, dx_near, dx_far)
+    grad_in, grad_out, gg = sum_stage(got)
     return (
         section_grad.reshape(shape),
         grad_in[None],

time: 53.8 us -> 53.8 us (level)
  waiting for transfers between devices: 8.97 us -> 8.26 us
  Pallas kernels: 8.84 us -> 9.49 us
    all_to_all x1, waiting for transfers between devices: 2.54 us -> 1.83 us  [per_device(): lax.all_to_all(part, 'dp', 0, 0, tiled=True, axis_index_groups=[SAMPLE_OR...]
    pallas_call x7 -> x8, Pallas kernels: 8.84 us -> 9.49 us  [call(): pl.pallas_call(kernel, out_shape=shapes, in_specs=[pl.BlockSpec(memory_sp...]
  transfers between devices with their start and end apart: 7 -> 7, of which waited for: 3 -> 3; matrix products, arithmetic and copies ran while one was open for 0% -> 0% of each run, Pallas kernels for 7% -> 9%
where the time goes in v8:
time: 53.8 us; the launch traced here: 53.3 us
  starting transfers between devices  34.8 us (65%)
  Pallas kernels  9.49 us (18%)
  waiting for transfers between devices  8.26 us (15%)
  between operations  0.73 us (1%)
    all_to_all x1, starting transfers between devices, per_device(): lax.all_to_all(part, 'dp', 0, 0, tiled=True, axis_index_groups=[SAMPLE_OR...  12.5 us
    ppermute x5, starting transfers between devices, sent(): return lax.ppermute(value, ('pipe', 'sg'), pairs)  12.4 us
    all_to_all x1, starting transfers between devices, per_device(): lax.all_to_all(pay, 'sg', 0, 0, tiled=True, axis_index_groups=[ORDER])  9.93 us
    pallas_call x8, Pallas kernels, call(): pl.pallas_call(kernel, out_shape=shapes, in_specs=[pl.BlockSpec(memory_sp...  9.49 us
    all_to_all x1, waiting for transfers between devices, per_device(): lax.all_to_all(pay, 'sg', 0, 0, tiled=True, axis_index_groups=[ORDER])  6.07 us
    all_to_all x1, waiting for transfers between devices, per_device(): lax.all_to_all(part, 'dp', 0, 0, tiled=True, axis_index_groups=[SAMPLE_OR...  1.83 us
  transfers between devices with their start and end apart: 7, of which 3 were waited for; matrix products, arithmetic and copies ran while one was open for 0% of the time, Pallas kernels for 9%

profile of v8, /device:TPU:2, one launch (start us, length us, event | category | flops | bytes accessed | tf_op | source)
XLA Modules:
  0.0 53.3 jit_solution(18300546291589235717)
XLA Ops:
  0.6 3.4 %collective-permute-start.1 = (bf16[256,256]{1,0:T(8,128)(2,1)}, bf16[256,256]{1,0:T(8,128)(2,1)S(1)}, u32[]{:S(2)}, u32[]{:S(2)}) collective-permute-start(bf16[256,256]{1,0:T(8,128)(2,1)} %bitcast.13), channel_id=1, source_target_pairs={{1,2},{2,1},{3,4},{4,3},{5,6},{6,5},{7,8},{8,7},{9,10},{10,9},{11,... | collective-permute-start | bytes 393224 | tf_op jit(solution)/shard_map/ppermute | solution.py:376
  4.0 5.1 %collective-permute-start = (bf16[256,256]{1,0:T(8,128)(2,1)}, bf16[256,256]{1,0:T(8,128)(2,1)S(1)}, u32[]{:S(2)}, u32[]{:S(2)}) collective-permute-start(bf16[256,256]{1,0:T(8,128)(2,1)} %bitcast.14), channel_id=1, source_target_pairs={{0,1},{1,0},{2,3},{3,2},{4,5},{5,4},{6,7},{7,6},{8,9},{9,8},{10,11... | collective-permute-start | bytes 393224 | tf_op jit(solution)/shard_map/ppermute | solution.py:376
  9.1 2.1 %shard_map.84 = (f32[256,256]{1,0:T(8,128)S(1)}, bf16[256,256]{1,0:T(8,128)(2,1)S(1)}, bf16[256,256]{1,0:T(8,128)(2,1)S(1)}, bf16[6912,256]{1,0:T(8,128)(2,1)S(1...) custom-call(bf16[256,256]{1,0:T(8,128)(2,1)} %bitcast.15, ...), custom_call_target="tpu_custom_call" | custom-call | flops 369098752 | bytes 5353472 | tf_op jit(solution)/shard_map/pallas_call | solution.py:278
  11.2 0.0 collective-permute-done.1.far
  11.2 0.7 %shard_map.85 = (bf16[256,256]{1,0:T(8,128)(2,1)S(1)}, f32[256,256]{1,0:T(8,128)S(1)}, f32[256,256]{1,0:T(8,128)S(1)}, bf16[256,256]{1,0:T(8,128)(2,1)S(1)}) custom-call(bf16[256,256]{1,0:T(8,128)(2,1)S(1)} %collective-permute-done.1.far, bf16[256,256]{1,0:T(8,128)(2,1)S(1)} %get-tuple-element.25.w_in, bf16[6912,256]{1,0:T(8,128)(2,1)S(1)} %get-tuple-element.26.wd, ...), custom_call_target="tpu_custom_call" | custom-call | flops 335544320 | bytes 4849664 | tf_op jit(solution)/shard_map/pallas_call | solution.py:278
  11.9 0.4 collective-permute-done.near
  12.3 4.1 %shard_map.86 = (bf16[256,256]{1,0:T(8,128)(2,1)S(1)}, bf16[256,256]{1,0:T(8,128)(2,1)S(1)}, bf16[256,256]{1,0:T(8,128)(2,1)S(1)}, bf16[32,8,768]{2,1,0:T(8,128)(2,1)}) custom-call(bf16[256,256]{1,0:T(8,128)(2,1)S(1)} %collective-permute-done.near, bf16[256,256]{1,0:T(8,128)(2,1)S(1)} %get-tuple-element.28.far_t, bf16[256,256]{1,0:T(8,128)(2,1)S(1)} %get-tuple-element.29.xt, ...), custom_call_target="tpu_custom_call" | custom-call | flops 2348810240 | bytes 6160384 | tf_op jit(solution)/shard_map/pallas_call | solution.py:278
  16.4 9.9 %all-to-all-start = ((bf16[32,8,768]{2,1,0:T(8,128)(2,1)}), bf16[32,8,768]{2,1,0:T(8,128)(2,1)S(1)}, u32[]{:S(2)}, u32[]{:S(2)}) async-start(bf16[32,8,768]{2,1,0:T(8,128)(2,1)} %get-tuple-element.42), calls=%async_computation | async-start | bytes 786432 | tf_op jit(solution)/shard_map/all_to_all | solution.py:398
  26.3 0.3 shard_map.88
  26.6 1.3 %collective-permute-start.3 = (bf16[256,256]{1,0:T(8,128)(2,1)S(1)}, bf16[256,256]{1,0:T(8,128)(2,1)S(1)}, u32[]{:S(2)}, u32[]{:S(2)}) collective-permute-start(bf16[256,256]{1,0:T(8,128)(2,1)S(1)} %get-tuple-element.40), channel_id=1, source_target_pairs={{32,1},{33,0},{34,3},{35,2},{36,5},{37,4},{38,7},{39,6},{40,9},{41... | collective-permute-start | bytes 393224 | tf_op jit(solution)/shard_map/ppermute | solution.py:376
  27.9 0.2 shard_map.87
  28.1 1.3 %collective-permute-start.4 = (bf16[256,256]{1,0:T(8,128)(2,1)S(1)}, bf16[256,256]{1,0:T(8,128)(2,1)S(1)}, u32[]{:S(2)}, u32[]{:S(2)}) collective-permute-start(bf16[256,256]{1,0:T(8,128)(2,1)S(1)} %get-tuple-element.41), channel_id=1, source_target_pairs={{33,2},{34,1},{35,4},{36,3},{37,6},{38,5},{39,8},{40,7},{41,10},{4... | collective-permute-start | bytes 393224 | tf_op jit(solution)/shard_map/ppermute | solution.py:376
  29.4 1.3 %collective-permute-start.2 = (bf16[256,256]{1,0:T(8,128)(2,1)S(1)}, bf16[256,256]{1,0:T(8,128)(2,1)S(1)}, u32[]{:S(2)}, u32[]{:S(2)}) collective-permute-start(bf16[256,256]{1,0:T(8,128)(2,1)S(1)} %shard_map.87), channel_id=1, source_target_pairs={{32,0},{33,1},{34,2},{35,3},{36,4},{37,5},{38,6},{39,7},{40,8},{41... | collective-permute-start | bytes 393224 | tf_op jit(solution)/shard_map/ppermute | solution.py:376
  30.7 6.1 %all-to-all-done.got = bf16[32,8,768]{2,1,0:T(8,128)(2,1)S(1)} async-done(((bf16[32,8,768]{2,1,0:T(8,128)(2,1)}), bf16[32,8,768]{2,1,0:T(8,128)(2,1)S(1)}, u32[]{:S(2)}, u32[]{:S(2)}) %all-to-all-start) | async-done | bytes 393248 | tf_op jit(solution)/shard_map/all_to_all | solution.py:398
  36.8 0.7 %shard_map.90 = f32[4,8,384]{2,1,0:T(8,128)} custom-call(bf16[32,8,768]{2,1,0:T(8,128)(2,1)S(1)} %all-to-all-done.got), custom_call_target="tpu_custom_call" | custom-call | flops 1000 | bytes 442368 | tf_op jit(solution)/shard_map/pallas_call | solution.py:278
  37.4 12.5 %all-to-all-start.1 = ((f32[4,8,384]{2,1,0:T(8,128)}), f32[4,8,384]{2,1,0:T(8,128)S(1)}, u32[]{:S(2)}, u32[]{:S(2)}) async-start(f32[4,8,384]{2,1,0:T(8,128)} %shard_map.90), calls=%async_computation.1 | async-start | bytes 98304 | tf_op jit(solution)/shard_map/all_to_all | solution.py:399
  50.0 0.0 collective-permute-done.3.dx_near
  50.0 0.0 collective-permute-done.4.dx_far
  50.0 0.0 collective-permute-done.2.dx
  50.0 0.7 %shard_map.89 = bf16[256,256]{1,0:T(8,128)(2,1)} custom-call(bf16[256,256]{1,0:T(8,128)(2,1)S(1)} %collective-permute-done.2.dx, bf16[256,256]{1,0:T(8,128)(2,1)S(1)} %collective-permute-done.3.dx_near, bf16[256,256]{1,0:T(8,128)(2,1)S(1)} %collective-permute-done.4.dx_far), custom_call_target="tpu_custom_call" | custom-call | flops 1000 | bytes 524288 | tf_op jit(solution)/shard_map/pallas_call | solution.py:278
  50.7 1.8 %all-to-all-done.1.got = f32[4,8,384]{2,1,0:T(8,128)S(1)} async-done(((f32[4,8,384]{2,1,0:T(8,128)}), f32[4,8,384]{2,1,0:T(8,128)S(1)}, u32[]{:S(2)}, u32[]{:S(2)}) %all-to-all-start.1) | async-done | bytes 49184 | tf_op jit(solution)/shard_map/all_to_all | solution.py:399
  52.5 0.8 %shard_map.91 = (f32[2,256]{1,0:T(2,128)}, f32[2,256]{1,0:T(2,128)}, f32[216,8]{1,0:T(8,128)}) custom-call(f32[4,8,384]{2,1,0:T(8,128)S(1)} %all-to-all-done.1.got), custom_call_target="tpu_custom_call" | custom-call | flops 1000 | bytes 60160 | tf_op jit(solution)/shard_map/pallas_call | solution.py:278
Async XLA Ops:
  0.6 10.6 %collective-permute-start.1 = (bf16[256,256]{1,0:T(8,128)(2,1)}, bf16[256,256]{1,0:T(8,128)(2,1)S(1)}, u32[]{:S(2)}, u32[]{:S(2)}) collective-permute-start(bf16[256,256]{1,0:T(8,128)(2,1)} %bitcast.13), channel_id=1, source_target_pairs={{1,2},{2,1},{3,4},{4,3},{5,6},{6,5},{7,8},{8,7},{9,10},{10,9},{11,... | collective-permute-start | bytes 393224 | tf_op jit(solution)/shard_map/ppermute | solution.py:376
  4.0 8.2 %collective-permute-start = (bf16[256,256]{1,0:T(8,128)(2,1)}, bf16[256,256]{1,0:T(8,128)(2,1)S(1)}, u32[]{:S(2)}, u32[]{:S(2)}) collective-permute-start(bf16[256,256]{1,0:T(8,128)(2,1)} %bitcast.14), channel_id=1, source_target_pairs={{0,1},{1,0},{2,3},{3,2},{4,5},{5,4},{6,7},{7,6},{8,9},{9,8},{10,11... | collective-permute-start | bytes 393224 | tf_op jit(solution)/shard_map/ppermute | solution.py:376
  16.4 20.4 %all-to-all-start = ((bf16[32,8,768]{2,1,0:T(8,128)(2,1)}), bf16[32,8,768]{2,1,0:T(8,128)(2,1)S(1)}, u32[]{:S(2)}, u32[]{:S(2)}) async-start(bf16[32,8,768]{2,1,0:T(8,128)(2,1)} %get-tuple-element.42), calls=%async_computation | async-start | bytes 786432 | tf_op jit(solution)/shard_map/all_to_all | solution.py:398
  26.6 23.4 %collective-permute-start.3 = (bf16[256,256]{1,0:T(8,128)(2,1)S(1)}, bf16[256,256]{1,0:T(8,128)(2,1)S(1)}, u32[]{:S(2)}, u32[]{:S(2)}) collective-permute-start(bf16[256,256]{1,0:T(8,128)(2,1)S(1)} %get-tuple-element.40), channel_id=1, source_target_pairs={{32,1},{33,0},{34,3},{35,2},{36,5},{37,4},{38,7},{39,6},{40,9},{41... | collective-permute-start | bytes 393224 | tf_op jit(solution)/shard_map/ppermute | solution.py:376
  28.1 21.9 %collective-permute-start.4 = (bf16[256,256]{1,0:T(8,128)(2,1)S(1)}, bf16[256,256]{1,0:T(8,128)(2,1)S(1)}, u32[]{:S(2)}, u32[]{:S(2)}) collective-permute-start(bf16[256,256]{1,0:T(8,128)(2,1)S(1)} %get-tuple-element.41), channel_id=1, source_target_pairs={{33,2},{34,1},{35,4},{36,3},{37,6},{38,5},{39,8},{40,7},{41,10},{4... | collective-permute-start | bytes 393224 | tf_op jit(solution)/shard_map/ppermute | solution.py:376
  29.4 20.6 %collective-permute-start.2 = (bf16[256,256]{1,0:T(8,128)(2,1)S(1)}, bf16[256,256]{1,0:T(8,128)(2,1)S(1)}, u32[]{:S(2)}, u32[]{:S(2)}) collective-permute-start(bf16[256,256]{1,0:T(8,128)(2,1)S(1)} %shard_map.87), channel_id=1, source_target_pairs={{32,0},{33,1},{34,2},{35,3},{36,4},{37,5},{38,6},{39,7},{40,8},{41... | collective-permute-start | bytes 393224 | tf_op jit(solution)/shard_map/ppermute | solution.py:376
  37.4 15.1 %all-to-all-start.1 = ((f32[4,8,384]{2,1,0:T(8,128)}), f32[4,8,384]{2,1,0:T(8,128)S(1)}, u32[]{:S(2)}, u32[]{:S(2)}) async-start(f32[4,8,384]{2,1,0:T(8,128)} %shard_map.90), calls=%async_computation.1 | async-start | bytes 98304 | tf_op jit(solution)/shard_map/all_to_all | solution.py:399
